TPU v7x, 256 devices: a whole 4x4x8 slice. The times are simulated.
256 devices in a mesh: blk: 32 (over x_lo, z, core), cd: 8 (over x_hi, y).
Axes of the slice: x: 4 (x_hi: 2, x_lo: 2; x = x_hi * 2 + x_lo), y: 4, z: 8, core: 2. Of those that a mesh axis runs over, the one named last changes fastest.
Arguments:
- t2_amps: bfloat16 [2048, 32768], P('blk', 'cd'), may hold values from -6 to 6
- integrals: bfloat16 [1024, 64, 4096], P('blk', None, 'cd'), may hold values from -0.09375 to 0.09375
- ab_sym: int32 [1024], P('blk'), may hold values from 0 to 7, as said below
- cd_sym: int32 [512], P('cd'), may hold values from 0 to 7, as said below
Outputs:
- ladder: bfloat16 [2048, 65536], P('cd', 'blk')
Inputs may be any that keep to these rules, and one draw needn't show every extreme that they name: `ab_sym`: each aligned block of 32 ab tiles (the tiles of one index of blk) holds exactly 4 tiles of every irreducible representation. `cd_sym`: each group of 64 consecutive cd tiles holds exactly 8 tiles of every irreducible representation.
All inputs are finite; a program needn't handle non-finite values.
Results may differ from a plain program's by a relative error of at most 0.015.
Values may be sent and summed in bfloat16 or wider, within the bound.
A program may use at most 128 MiB of HBM per device.

v0:
```python
import jax
import jax.numpy as jnp
from jax import lax
from jax.sharding import PartitionSpec as P

NSYM = 8


def shifted(x, axis, by):
    length = lax.axis_size(axis)
    return lax.ppermute(x, axis, [(i, (i + by) % length) for i in range(length)])


def per_device(t2_amps, integrals, ab_sym, cd_sym):
    loop_len = lax.axis_size("blk")
    my_index = lax.axis_index("blk")
    block_rows = t2_amps.shape[0]
    ab_tiles = integrals.shape[0]
    tile_width = integrals.shape[1]
    packed = integrals.shape[2]
    cd_tiles = cd_sym.shape[0]
    order_ab = jnp.argsort(ab_sym, stable=True)
    inverse_ab = jnp.argsort(order_ab, stable=True)
    order_cd = jnp.argsort(cd_sym, stable=True)
    ints_sorted = jnp.take(integrals, order_ab, axis=0).reshape(
        NSYM, ab_tiles * tile_width // NSYM, packed
    )
    own_block = jnp.take(t2_amps.reshape(block_rows, cd_tiles, tile_width), order_cd, axis=1)
    own_block = own_block.reshape(block_rows, cd_tiles * tile_width)

    def contract(t2_block):
        rows = t2_block.shape[0]
        grouped = t2_block.reshape(rows, NSYM, packed)
        product = jnp.einsum(
            "isk,smk->ism", grouped, ints_sorted, preferred_element_type=jnp.float32
        )
        return product.reshape(rows, ab_tiles * tile_width).astype(jnp.bfloat16)

    def place(buffer, t2_block, offset):
        row_first = (my_index - offset) % loop_len * block_rows
        return lax.dynamic_update_slice_in_dim(buffer, contract(t2_block), row_first, 0)

    empty_buf = jnp.zeros((loop_len * block_rows, ab_tiles * tile_width), jnp.bfloat16)
    first_buf = place(empty_buf, own_block, 0)

    def one_turn(offset, carry):
        moving, buffer = carry
        moving = shifted(moving, "blk", 1)
        return (moving, place(buffer, moving, offset))

    _, partial_value = lax.fori_loop(1, loop_len, one_turn, (own_block, first_buf))
    summed = lax.psum_scatter(partial_value, "cd", scatter_dimension=0, tiled=True).astype(
        jnp.float32
    )
    out_rows = summed.shape[0]
    summed = jnp.take(summed.reshape(out_rows, ab_tiles, tile_width), inverse_ab, axis=1)
    return summed.reshape(out_rows, ab_tiles * tile_width).astype(jnp.bfloat16)


def solution(mesh):
    in_specs = (P("blk", "cd"), P("blk", None, "cd"), P("blk"), P("cd"))
    out_specs = P("cd", "blk")
    return jax.shard_map(
        per_device, mesh=mesh, in_specs=in_specs, out_specs=out_specs, check_vma=False
    )
```

profile of v0, /device:TPU:17, one launch (start us, length us, event | category | flops | bytes accessed | tf_op | source)
XLA Modules:
  0.0 606.9 jit_solution(14905567775946811492)
XLA Ops:
  6.5 2.8 sort.50
  11.7 2.8 reshape.61
  30.9 3.2 copy-done.2
  34.1 425.9 %while.17 = (s32[]{:T(128)}, bf16[64,4096]{1,0:T(8,128)(2,1)S(1)}, bf16[2048,2048]{1,0:T(8,128)(2,1)}, bf16[8,256,512]{2,1,0:T(8,128)(2,1)}, s32[]{:T(128)}, /*i...) while((s32[]{:T(128)}, bf16[64,4096]{1,0:T(8,128)(2,1)S(1)}, ...), condition=%wide.region_4.5_spmd, body=%wide.region_3.4_spmd.sunk | while | flops 134348800 | bytes 7078208 | solution.py:51
  36.3 6.1 %collective-permute-done = bf16[64,4096]{1,0:T(8,128)(2,1)S(1)} collective-permute-done((bf16[64,4096]{1,0:T(8,128)(2,1)S(1)}, bf16[64,4096]{1,0:T(8,128)(2,1)S(1)}, u32[]{:S(2)}, u32[]{:S(2)}) %collective-permute-start) | collective-permute-done | bytes 524320 | tf_op jit(solution)/shard_map/while/body/eval_jaxpr/ppermute | solution.py:11
  45.6 2.6 collective-permute-start
  48.1 6.1 %collective-permute-done = bf16[64,4096]{1,0:T(8,128)(2,1)S(1)} collective-permute-done((bf16[64,4096]{1,0:T(8,128)(2,1)S(1)}, bf16[64,4096]{1,0:T(8,128)(2,1)S(1)}, u32[]{:S(2)}, u32[]{:S(2)}) %collective-permute-start) | collective-permute-done | bytes 524320 | tf_op jit(solution)/shard_map/while/body/eval_jaxpr/ppermute | solution.py:11
  57.4 2.5 collective-permute-start
  59.9 6.5 %collective-permute-done = bf16[64,4096]{1,0:T(8,128)(2,1)S(1)} collective-permute-done((bf16[64,4096]{1,0:T(8,128)(2,1)S(1)}, bf16[64,4096]{1,0:T(8,128)(2,1)S(1)}, u32[]{:S(2)}, u32[]{:S(2)}) %collective-permute-start) | collective-permute-done | bytes 524320 | tf_op jit(solution)/shard_map/while/body/eval_jaxpr/ppermute | solution.py:11
  71.8 8.6 %collective-permute-done = bf16[64,4096]{1,0:T(8,128)(2,1)S(1)} collective-permute-done((bf16[64,4096]{1,0:T(8,128)(2,1)S(1)}, bf16[64,4096]{1,0:T(8,128)(2,1)S(1)}, u32[]{:S(2)}, u32[]{:S(2)}) %collective-permute-start) | collective-permute-done | bytes 524320 | tf_op jit(solution)/shard_map/while/body/eval_jaxpr/ppermute | solution.py:11
  83.6 10.7 %collective-permute-done = bf16[64,4096]{1,0:T(8,128)(2,1)S(1)} collective-permute-done((bf16[64,4096]{1,0:T(8,128)(2,1)S(1)}, bf16[64,4096]{1,0:T(8,128)(2,1)S(1)}, u32[]{:S(2)}, u32[]{:S(2)}) %collective-permute-start) | collective-permute-done | bytes 524320 | tf_op jit(solution)/shard_map/while/body/eval_jaxpr/ppermute | solution.py:11
  97.6 10.7 %collective-permute-done = bf16[64,4096]{1,0:T(8,128)(2,1)S(1)} collective-permute-done((bf16[64,4096]{1,0:T(8,128)(2,1)S(1)}, bf16[64,4096]{1,0:T(8,128)(2,1)S(1)}, u32[]{:S(2)}, u32[]{:S(2)}) %collective-permute-start) | collective-permute-done | bytes 524320 | tf_op jit(solution)/shard_map/while/body/eval_jaxpr/ppermute | solution.py:11
  108.2 2.3 fusion.13
  111.5 10.7 %collective-permute-done = bf16[64,4096]{1,0:T(8,128)(2,1)S(1)} collective-permute-done((bf16[64,4096]{1,0:T(8,128)(2,1)S(1)}, bf16[64,4096]{1,0:T(8,128)(2,1)S(1)}, u32[]{:S(2)}, u32[]{:S(2)}) %collective-permute-start) | collective-permute-done | bytes 524320 | tf_op jit(solution)/shard_map/while/body/eval_jaxpr/ppermute | solution.py:11
  125.5 10.7 %collective-permute-done = bf16[64,4096]{1,0:T(8,128)(2,1)S(1)} collective-permute-done((bf16[64,4096]{1,0:T(8,128)(2,1)S(1)}, bf16[64,4096]{1,0:T(8,128)(2,1)S(1)}, u32[]{:S(2)}, u32[]{:S(2)}) %collective-permute-start) | collective-permute-done | bytes 524320 | tf_op jit(solution)/shard_map/while/body/eval_jaxpr/ppermute | solution.py:11
  139.4 10.7 %collective-permute-done = bf16[64,4096]{1,0:T(8,128)(2,1)S(1)} collective-permute-done((bf16[64,4096]{1,0:T(8,128)(2,1)S(1)}, bf16[64,4096]{1,0:T(8,128)(2,1)S(1)}, u32[]{:S(2)}, u32[]{:S(2)}) %collective-permute-start) | collective-permute-done | bytes 524320 | tf_op jit(solution)/shard_map/while/body/eval_jaxpr/ppermute | solution.py:11
  150.1 2.3 fusion.13
  153.3 10.7 %collective-permute-done = bf16[64,4096]{1,0:T(8,128)(2,1)S(1)} collective-permute-done((bf16[64,4096]{1,0:T(8,128)(2,1)S(1)}, bf16[64,4096]{1,0:T(8,128)(2,1)S(1)}, u32[]{:S(2)}, u32[]{:S(2)}) %collective-permute-start) | collective-permute-done | bytes 524320 | tf_op jit(solution)/shard_map/while/body/eval_jaxpr/ppermute | solution.py:11
  164.0 2.3 fusion.13
  167.3 10.7 %collective-permute-done = bf16[64,4096]{1,0:T(8,128)(2,1)S(1)} collective-permute-done((bf16[64,4096]{1,0:T(8,128)(2,1)S(1)}, bf16[64,4096]{1,0:T(8,128)(2,1)S(1)}, u32[]{:S(2)}, u32[]{:S(2)}) %collective-permute-start) | collective-permute-done | bytes 524320 | tf_op jit(solution)/shard_map/while/body/eval_jaxpr/ppermute | solution.py:11
  178.0 2.3 fusion.13
  181.2 10.7 %collective-permute-done = bf16[64,4096]{1,0:T(8,128)(2,1)S(1)} collective-permute-done((bf16[64,4096]{1,0:T(8,128)(2,1)S(1)}, bf16[64,4096]{1,0:T(8,128)(2,1)S(1)}, u32[]{:S(2)}, u32[]{:S(2)}) %collective-permute-start) | collective-permute-done | bytes 524320 | tf_op jit(solution)/shard_map/while/body/eval_jaxpr/ppermute | solution.py:11
  195.2 10.7 %collective-permute-done = bf16[64,4096]{1,0:T(8,128)(2,1)S(1)} collective-permute-done((bf16[64,4096]{1,0:T(8,128)(2,1)S(1)}, bf16[64,4096]{1,0:T(8,128)(2,1)S(1)}, u32[]{:S(2)}, u32[]{:S(2)}) %collective-permute-start) | collective-permute-done | bytes 524320 | tf_op jit(solution)/shard_map/while/body/eval_jaxpr/ppermute | solution.py:11
  209.1 10.7 %collective-permute-done = bf16[64,4096]{1,0:T(8,128)(2,1)S(1)} collective-permute-done((bf16[64,4096]{1,0:T(8,128)(2,1)S(1)}, bf16[64,4096]{1,0:T(8,128)(2,1)S(1)}, u32[]{:S(2)}, u32[]{:S(2)}) %collective-permute-start) | collective-permute-done | bytes 524320 | tf_op jit(solution)/shard_map/while/body/eval_jaxpr/ppermute | solution.py:11
  223.1 10.7 %collective-permute-done = bf16[64,4096]{1,0:T(8,128)(2,1)S(1)} collective-permute-done((bf16[64,4096]{1,0:T(8,128)(2,1)S(1)}, bf16[64,4096]{1,0:T(8,128)(2,1)S(1)}, u32[]{:S(2)}, u32[]{:S(2)}) %collective-permute-start) | collective-permute-done | bytes 524320 | tf_op jit(solution)/shard_map/while/body/eval_jaxpr/ppermute | solution.py:11
  237.0 10.7 %collective-permute-done = bf16[64,4096]{1,0:T(8,128)(2,1)S(1)} collective-permute-done((bf16[64,4096]{1,0:T(8,128)(2,1)S(1)}, bf16[64,4096]{1,0:T(8,128)(2,1)S(1)}, u32[]{:S(2)}, u32[]{:S(2)}) %collective-permute-start) | collective-permute-done | bytes 524320 | tf_op jit(solution)/shard_map/while/body/eval_jaxpr/ppermute | solution.py:11
  251.0 10.7 %collective-permute-done = bf16[64,4096]{1,0:T(8,128)(2,1)S(1)} collective-permute-done((bf16[64,4096]{1,0:T(8,128)(2,1)S(1)}, bf16[64,4096]{1,0:T(8,128)(2,1)S(1)}, u32[]{:S(2)}, u32[]{:S(2)}) %collective-permute-start) | collective-permute-done | bytes 524320 | tf_op jit(solution)/shard_map/while/body/eval_jaxpr/ppermute | solution.py:11
  261.6 2.3 fusion.13
  264.9 10.7 %collective-permute-done = bf16[64,4096]{1,0:T(8,128)(2,1)S(1)} collective-permute-done((bf16[64,4096]{1,0:T(8,128)(2,1)S(1)}, bf16[64,4096]{1,0:T(8,128)(2,1)S(1)}, u32[]{:S(2)}, u32[]{:S(2)}) %collective-permute-start) | collective-permute-done | bytes 524320 | tf_op jit(solution)/shard_map/while/body/eval_jaxpr/ppermute | solution.py:11
  275.6 2.3 fusion.13
  278.8 10.7 %collective-permute-done = bf16[64,4096]{1,0:T(8,128)(2,1)S(1)} collective-permute-done((bf16[64,4096]{1,0:T(8,128)(2,1)S(1)}, bf16[64,4096]{1,0:T(8,128)(2,1)S(1)}, u32[]{:S(2)}, u32[]{:S(2)}) %collective-permute-start) | collective-permute-done | bytes 524320 | tf_op jit(solution)/shard_map/while/body/eval_jaxpr/ppermute | solution.py:11
  292.7 10.7 %collective-permute-done = bf16[64,4096]{1,0:T(8,128)(2,1)S(1)} collective-permute-done((bf16[64,4096]{1,0:T(8,128)(2,1)S(1)}, bf16[64,4096]{1,0:T(8,128)(2,1)S(1)}, u32[]{:S(2)}, u32[]{:S(2)}) %collective-permute-start) | collective-permute-done | bytes 524320 | tf_op jit(solution)/shard_map/while/body/eval_jaxpr/ppermute | solution.py:11
  306.7 10.7 %collective-permute-done = bf16[64,4096]{1,0:T(8,128)(2,1)S(1)} collective-permute-done((bf16[64,4096]{1,0:T(8,128)(2,1)S(1)}, bf16[64,4096]{1,0:T(8,128)(2,1)S(1)}, u32[]{:S(2)}, u32[]{:S(2)}) %collective-permute-start) | collective-permute-done | bytes 524320 | tf_op jit(solution)/shard_map/while/body/eval_jaxpr/ppermute | solution.py:11
  320.7 10.7 %collective-permute-done = bf16[64,4096]{1,0:T(8,128)(2,1)S(1)} collective-permute-done((bf16[64,4096]{1,0:T(8,128)(2,1)S(1)}, bf16[64,4096]{1,0:T(8,128)(2,1)S(1)}, u32[]{:S(2)}, u32[]{:S(2)}) %collective-permute-start) | collective-permute-done | bytes 524320 | tf_op jit(solution)/shard_map/while/body/eval_jaxpr/ppermute | solution.py:11
  334.6 10.7 %collective-permute-done = bf16[64,4096]{1,0:T(8,128)(2,1)S(1)} collective-permute-done((bf16[64,4096]{1,0:T(8,128)(2,1)S(1)}, bf16[64,4096]{1,0:T(8,128)(2,1)S(1)}, u32[]{:S(2)}, u32[]{:S(2)}) %collective-permute-start) | collective-permute-done | bytes 524320 | tf_op jit(solution)/shard_map/while/body/eval_jaxpr/ppermute | solution.py:11
  348.5 10.7 %collective-permute-done = bf16[64,4096]{1,0:T(8,128)(2,1)S(1)} collective-permute-done((bf16[64,4096]{1,0:T(8,128)(2,1)S(1)}, bf16[64,4096]{1,0:T(8,128)(2,1)S(1)}, u32[]{:S(2)}, u32[]{:S(2)}) %collective-permute-start) | collective-permute-done | bytes 524320 | tf_op jit(solution)/shard_map/while/body/eval_jaxpr/ppermute | solution.py:11
  362.5 10.7 %collective-permute-done = bf16[64,4096]{1,0:T(8,128)(2,1)S(1)} collective-permute-done((bf16[64,4096]{1,0:T(8,128)(2,1)S(1)}, bf16[64,4096]{1,0:T(8,128)(2,1)S(1)}, u32[]{:S(2)}, u32[]{:S(2)}) %collective-permute-start) | collective-permute-done | bytes 524320 | tf_op jit(solution)/shard_map/while/body/eval_jaxpr/ppermute | solution.py:11
  373.2 2.3 fusion.13
  376.5 10.7 %collective-permute-done = bf16[64,4096]{1,0:T(8,128)(2,1)S(1)} collective-permute-done((bf16[64,4096]{1,0:T(8,128)(2,1)S(1)}, bf16[64,4096]{1,0:T(8,128)(2,1)S(1)}, u32[]{:S(2)}, u32[]{:S(2)}) %collective-permute-start) | collective-permute-done | bytes 524320 | tf_op jit(solution)/shard_map/while/body/eval_jaxpr/ppermute | solution.py:11
  390.4 10.7 %collective-permute-done = bf16[64,4096]{1,0:T(8,128)(2,1)S(1)} collective-permute-done((bf16[64,4096]{1,0:T(8,128)(2,1)S(1)}, bf16[64,4096]{1,0:T(8,128)(2,1)S(1)}, u32[]{:S(2)}, u32[]{:S(2)}) %collective-permute-start) | collective-permute-done | bytes 524320 | tf_op jit(solution)/shard_map/while/body/eval_jaxpr/ppermute | solution.py:11
  404.3 10.7 %collective-permute-done = bf16[64,4096]{1,0:T(8,128)(2,1)S(1)} collective-permute-done((bf16[64,4096]{1,0:T(8,128)(2,1)S(1)}, bf16[64,4096]{1,0:T(8,128)(2,1)S(1)}, u32[]{:S(2)}, u32[]{:S(2)}) %collective-permute-start) | collective-permute-done | bytes 524320 | tf_op jit(solution)/shard_map/while/body/eval_jaxpr/ppermute | solution.py:11
  415.0 2.3 fusion.13
  418.3 10.7 %collective-permute-done = bf16[64,4096]{1,0:T(8,128)(2,1)S(1)} collective-permute-done((bf16[64,4096]{1,0:T(8,128)(2,1)S(1)}, bf16[64,4096]{1,0:T(8,128)(2,1)S(1)}, u32[]{:S(2)}, u32[]{:S(2)}) %collective-permute-start) | collective-permute-done | bytes 524320 | tf_op jit(solution)/shard_map/while/body/eval_jaxpr/ppermute | solution.py:11
  429.0 2.3 fusion.13
  432.2 10.7 %collective-permute-done = bf16[64,4096]{1,0:T(8,128)(2,1)S(1)} collective-permute-done((bf16[64,4096]{1,0:T(8,128)(2,1)S(1)}, bf16[64,4096]{1,0:T(8,128)(2,1)S(1)}, u32[]{:S(2)}, u32[]{:S(2)}) %collective-permute-start) | collective-permute-done | bytes 524320 | tf_op jit(solution)/shard_map/while/body/eval_jaxpr/ppermute | solution.py:11
  446.2 10.7 %collective-permute-done = bf16[64,4096]{1,0:T(8,128)(2,1)S(1)} collective-permute-done((bf16[64,4096]{1,0:T(8,128)(2,1)S(1)}, bf16[64,4096]{1,0:T(8,128)(2,1)S(1)}, u32[]{:S(2)}, u32[]{:S(2)}) %collective-permute-start) | collective-permute-done | bytes 524320 | tf_op jit(solution)/shard_map/while/body/eval_jaxpr/ppermute | solution.py:11
  460.0 12.4 %copy.19 = bf16[2048,2048]{0,1:T(8,128)(2,1)} copy(bf16[2048,2048]{1,0:T(8,128)(2,1)} %get-tuple-element.144) | data formatting | bytes 16777216 | tf_op jit(solution)/shard_map/while | solution.py:51
  474.2 120.4 %reduce-scatter.2.cloned.1.call-done = bf16[256,2048]{0,1:T(8,128)(2,1)} async-done(((bf16[2048,2048]{0,1:T(8,128)(2,1)}), bf16[256,2048]{0,1:T(8,128)(2,1)}) %reduce-scatter.2.cloned.1.call-update) | async-done | bytes 1048592 | tf_op jit(solution)/shard_map/reduce_scatter | solution.py:52
  (195 shorter events, 108.3 us)
Async XLA Ops:
  6.5 17.1 %copy-start = (bf16[32,64,512]{2,1,0:T(8,128)(2,1)S(1)}, bf16[32,64,512]{2,1,0:T(8,128)(2,1)}, u32[]{:S(2)}) copy-start(bf16[32,64,512]{2,1,0:T(8,128)(2,1)} %param.7) | copy-start | bytes 6291460
  6.5 588.0 %reduce-scatter.2.cloned.1.call-start = ((), (), s32[]{:S(2)}) async-start(), calls=%async_computation.1 | async-start | bytes 9437184 | tf_op jit(solution)/shard_map/reduce_scatter | solution.py:52
  25.7 1.8 copy-start.4
  27.5 1.4 copy-start.1
  27.5 2.2 copy-start.3
  30.9 3.2 copy-start.2
  34.1 8.3 %collective-permute-start = (bf16[64,4096]{1,0:T(8,128)(2,1)S(1)}, bf16[64,4096]{1,0:T(8,128)(2,1)S(1)}, u32[]{:S(2)}, u32[]{:S(2)}) collective-permute-start(bf16[64,4096]{1,0:T(8,128)(2,1)S(1)} %get-tuple-element.198), channel_id=1, source_target_pairs={{0,8},{8,16},{16,24},{24,32},{32,40},{40,48},{48,56},{56,64},{64,7... | collective-permute-start | bytes 1572872 | tf_op jit(solution)/shard_map/while/body/eval_jaxpr/ppermute | solution.py:11
  45.6 8.7 %collective-permute-start = (bf16[64,4096]{1,0:T(8,128)(2,1)S(1)}, bf16[64,4096]{1,0:T(8,128)(2,1)S(1)}, u32[]{:S(2)}, u32[]{:S(2)}) collective-permute-start(bf16[64,4096]{1,0:T(8,128)(2,1)S(1)} %get-tuple-element.198), channel_id=1, source_target_pairs={{0,8},{8,16},{16,24},{24,32},{32,40},{40,48},{48,56},{56,64},{64,7... | collective-permute-start | bytes 1572872 | tf_op jit(solution)/shard_map/while/body/eval_jaxpr/ppermute | solution.py:11
  57.4 9.0 %collective-permute-start = (bf16[64,4096]{1,0:T(8,128)(2,1)S(1)}, bf16[64,4096]{1,0:T(8,128)(2,1)S(1)}, u32[]{:S(2)}, u32[]{:S(2)}) collective-permute-start(bf16[64,4096]{1,0:T(8,128)(2,1)S(1)} %get-tuple-element.198), channel_id=1, source_target_pairs={{0,8},{8,16},{16,24},{24,32},{32,40},{40,48},{48,56},{56,64},{64,7... | collective-permute-start | bytes 1572872 | tf_op jit(solution)/shard_map/while/body/eval_jaxpr/ppermute | solution.py:11
  69.6 10.8 %collective-permute-start = (bf16[64,4096]{1,0:T(8,128)(2,1)S(1)}, bf16[64,4096]{1,0:T(8,128)(2,1)S(1)}, u32[]{:S(2)}, u32[]{:S(2)}) collective-permute-start(bf16[64,4096]{1,0:T(8,128)(2,1)S(1)} %get-tuple-element.198), channel_id=1, source_target_pairs={{0,8},{8,16},{16,24},{24,32},{32,40},{40,48},{48,56},{56,64},{64,7... | collective-permute-start | bytes 1572872 | tf_op jit(solution)/shard_map/while/body/eval_jaxpr/ppermute | solution.py:11
  83.5 10.8 %collective-permute-start = (bf16[64,4096]{1,0:T(8,128)(2,1)S(1)}, bf16[64,4096]{1,0:T(8,128)(2,1)S(1)}, u32[]{:S(2)}, u32[]{:S(2)}) collective-permute-start(bf16[64,4096]{1,0:T(8,128)(2,1)S(1)} %get-tuple-element.198), channel_id=1, source_target_pairs={{0,8},{8,16},{16,24},{24,32},{32,40},{40,48},{48,56},{56,64},{64,7... | collective-permute-start | bytes 1572872 | tf_op jit(solution)/shard_map/while/body/eval_jaxpr/ppermute | solution.py:11
  97.4 10.8 %collective-permute-start = (bf16[64,4096]{1,0:T(8,128)(2,1)S(1)}, bf16[64,4096]{1,0:T(8,128)(2,1)S(1)}, u32[]{:S(2)}, u32[]{:S(2)}) collective-permute-start(bf16[64,4096]{1,0:T(8,128)(2,1)S(1)} %get-tuple-element.198), channel_id=1, source_target_pairs={{0,8},{8,16},{16,24},{24,32},{32,40},{40,48},{48,56},{56,64},{64,7... | collective-permute-start | bytes 1572872 | tf_op jit(solution)/shard_map/while/body/eval_jaxpr/ppermute | solution.py:11
  111.4 10.8 %collective-permute-start = (bf16[64,4096]{1,0:T(8,128)(2,1)S(1)}, bf16[64,4096]{1,0:T(8,128)(2,1)S(1)}, u32[]{:S(2)}, u32[]{:S(2)}) collective-permute-start(bf16[64,4096]{1,0:T(8,128)(2,1)S(1)} %get-tuple-element.198), channel_id=1, source_target_pairs={{0,8},{8,16},{16,24},{24,32},{32,40},{40,48},{48,56},{56,64},{64,7... | collective-permute-start | bytes 1572872 | tf_op jit(solution)/shard_map/while/body/eval_jaxpr/ppermute | solution.py:11
  125.4 10.8 %collective-permute-start = (bf16[64,4096]{1,0:T(8,128)(2,1)S(1)}, bf16[64,4096]{1,0:T(8,128)(2,1)S(1)}, u32[]{:S(2)}, u32[]{:S(2)}) collective-permute-start(bf16[64,4096]{1,0:T(8,128)(2,1)S(1)} %get-tuple-element.198), channel_id=1, source_target_pairs={{0,8},{8,16},{16,24},{24,32},{32,40},{40,48},{48,56},{56,64},{64,7... | collective-permute-start | bytes 1572872 | tf_op jit(solution)/shard_map/while/body/eval_jaxpr/ppermute | solution.py:11
  139.3 10.8 %collective-permute-start = (bf16[64,4096]{1,0:T(8,128)(2,1)S(1)}, bf16[64,4096]{1,0:T(8,128)(2,1)S(1)}, u32[]{:S(2)}, u32[]{:S(2)}) collective-permute-start(bf16[64,4096]{1,0:T(8,128)(2,1)S(1)} %get-tuple-element.198), channel_id=1, source_target_pairs={{0,8},{8,16},{16,24},{24,32},{32,40},{40,48},{48,56},{56,64},{64,7... | collective-permute-start | bytes 1572872 | tf_op jit(solution)/shard_map/while/body/eval_jaxpr/ppermute | solution.py:11
  153.2 10.8 %collective-permute-start = (bf16[64,4096]{1,0:T(8,128)(2,1)S(1)}, bf16[64,4096]{1,0:T(8,128)(2,1)S(1)}, u32[]{:S(2)}, u32[]{:S(2)}) collective-permute-start(bf16[64,4096]{1,0:T(8,128)(2,1)S(1)} %get-tuple-element.198), channel_id=1, source_target_pairs={{0,8},{8,16},{16,24},{24,32},{32,40},{40,48},{48,56},{56,64},{64,7... | collective-permute-start | bytes 1572872 | tf_op jit(solution)/shard_map/while/body/eval_jaxpr/ppermute | solution.py:11
  167.2 10.8 %collective-permute-start = (bf16[64,4096]{1,0:T(8,128)(2,1)S(1)}, bf16[64,4096]{1,0:T(8,128)(2,1)S(1)}, u32[]{:S(2)}, u32[]{:S(2)}) collective-permute-start(bf16[64,4096]{1,0:T(8,128)(2,1)S(1)} %get-tuple-element.198), channel_id=1, source_target_pairs={{0,8},{8,16},{16,24},{24,32},{32,40},{40,48},{48,56},{56,64},{64,7... | collective-permute-start | bytes 1572872 | tf_op jit(solution)/shard_map/while/body/eval_jaxpr/ppermute | solution.py:11
  181.1 10.8 %collective-permute-start = (bf16[64,4096]{1,0:T(8,128)(2,1)S(1)}, bf16[64,4096]{1,0:T(8,128)(2,1)S(1)}, u32[]{:S(2)}, u32[]{:S(2)}) collective-permute-start(bf16[64,4096]{1,0:T(8,128)(2,1)S(1)} %get-tuple-element.198), channel_id=1, source_target_pairs={{0,8},{8,16},{16,24},{24,32},{32,40},{40,48},{48,56},{56,64},{64,7... | collective-permute-start | bytes 1572872 | tf_op jit(solution)/shard_map/while/body/eval_jaxpr/ppermute | solution.py:11
  195.1 10.8 %collective-permute-start = (bf16[64,4096]{1,0:T(8,128)(2,1)S(1)}, bf16[64,4096]{1,0:T(8,128)(2,1)S(1)}, u32[]{:S(2)}, u32[]{:S(2)}) collective-permute-start(bf16[64,4096]{1,0:T(8,128)(2,1)S(1)} %get-tuple-element.198), channel_id=1, source_target_pairs={{0,8},{8,16},{16,24},{24,32},{32,40},{40,48},{48,56},{56,64},{64,7... | collective-permute-start | bytes 1572872 | tf_op jit(solution)/shard_map/while/body/eval_jaxpr/ppermute | solution.py:11
  209.0 10.8 %collective-permute-start = (bf16[64,4096]{1,0:T(8,128)(2,1)S(1)}, bf16[64,4096]{1,0:T(8,128)(2,1)S(1)}, u32[]{:S(2)}, u32[]{:S(2)}) collective-permute-start(bf16[64,4096]{1,0:T(8,128)(2,1)S(1)} %get-tuple-element.198), channel_id=1, source_target_pairs={{0,8},{8,16},{16,24},{24,32},{32,40},{40,48},{48,56},{56,64},{64,7... | collective-permute-start | bytes 1572872 | tf_op jit(solution)/shard_map/while/body/eval_jaxpr/ppermute | solution.py:11
  223.0 10.8 %collective-permute-start = (bf16[64,4096]{1,0:T(8,128)(2,1)S(1)}, bf16[64,4096]{1,0:T(8,128)(2,1)S(1)}, u32[]{:S(2)}, u32[]{:S(2)}) collective-permute-start(bf16[64,4096]{1,0:T(8,128)(2,1)S(1)} %get-tuple-element.198), channel_id=1, source_target_pairs={{0,8},{8,16},{16,24},{24,32},{32,40},{40,48},{48,56},{56,64},{64,7... | collective-permute-start | bytes 1572872 | tf_op jit(solution)/shard_map/while/body/eval_jaxpr/ppermute | solution.py:11
  236.9 10.8 %collective-permute-start = (bf16[64,4096]{1,0:T(8,128)(2,1)S(1)}, bf16[64,4096]{1,0:T(8,128)(2,1)S(1)}, u32[]{:S(2)}, u32[]{:S(2)}) collective-permute-start(bf16[64,4096]{1,0:T(8,128)(2,1)S(1)} %get-tuple-element.198), channel_id=1, source_target_pairs={{0,8},{8,16},{16,24},{24,32},{32,40},{40,48},{48,56},{56,64},{64,7... | collective-permute-start | bytes 1572872 | tf_op jit(solution)/shard_map/while/body/eval_jaxpr/ppermute | solution.py:11
  250.8 10.8 %collective-permute-start = (bf16[64,4096]{1,0:T(8,128)(2,1)S(1)}, bf16[64,4096]{1,0:T(8,128)(2,1)S(1)}, u32[]{:S(2)}, u32[]{:S(2)}) collective-permute-start(bf16[64,4096]{1,0:T(8,128)(2,1)S(1)} %get-tuple-element.198), channel_id=1, source_target_pairs={{0,8},{8,16},{16,24},{24,32},{32,40},{40,48},{48,56},{56,64},{64,7... | collective-permute-start | bytes 1572872 | tf_op jit(solution)/shard_map/while/body/eval_jaxpr/ppermute | solution.py:11
  264.7 10.8 %collective-permute-start = (bf16[64,4096]{1,0:T(8,128)(2,1)S(1)}, bf16[64,4096]{1,0:T(8,128)(2,1)S(1)}, u32[]{:S(2)}, u32[]{:S(2)}) collective-permute-start(bf16[64,4096]{1,0:T(8,128)(2,1)S(1)} %get-tuple-element.198), channel_id=1, source_target_pairs={{0,8},{8,16},{16,24},{24,32},{32,40},{40,48},{48,56},{56,64},{64,7... | collective-permute-start | bytes 1572872 | tf_op jit(solution)/shard_map/while/body/eval_jaxpr/ppermute | solution.py:11
  278.7 10.8 %collective-permute-start = (bf16[64,4096]{1,0:T(8,128)(2,1)S(1)}, bf16[64,4096]{1,0:T(8,128)(2,1)S(1)}, u32[]{:S(2)}, u32[]{:S(2)}) collective-permute-start(bf16[64,4096]{1,0:T(8,128)(2,1)S(1)} %get-tuple-element.198), channel_id=1, source_target_pairs={{0,8},{8,16},{16,24},{24,32},{32,40},{40,48},{48,56},{56,64},{64,7... | collective-permute-start | bytes 1572872 | tf_op jit(solution)/shard_map/while/body/eval_jaxpr/ppermute | solution.py:11
  292.6 10.8 %collective-permute-start = (bf16[64,4096]{1,0:T(8,128)(2,1)S(1)}, bf16[64,4096]{1,0:T(8,128)(2,1)S(1)}, u32[]{:S(2)}, u32[]{:S(2)}) collective-permute-start(bf16[64,4096]{1,0:T(8,128)(2,1)S(1)} %get-tuple-element.198), channel_id=1, source_target_pairs={{0,8},{8,16},{16,24},{24,32},{32,40},{40,48},{48,56},{56,64},{64,7... | collective-permute-start | bytes 1572872 | tf_op jit(solution)/shard_map/while/body/eval_jaxpr/ppermute | solution.py:11
  306.6 10.8 %collective-permute-start = (bf16[64,4096]{1,0:T(8,128)(2,1)S(1)}, bf16[64,4096]{1,0:T(8,128)(2,1)S(1)}, u32[]{:S(2)}, u32[]{:S(2)}) collective-permute-start(bf16[64,4096]{1,0:T(8,128)(2,1)S(1)} %get-tuple-element.198), channel_id=1, source_target_pairs={{0,8},{8,16},{16,24},{24,32},{32,40},{40,48},{48,56},{56,64},{64,7... | collective-permute-start | bytes 1572872 | tf_op jit(solution)/shard_map/while/body/eval_jaxpr/ppermute | solution.py:11
  320.6 10.8 %collective-permute-start = (bf16[64,4096]{1,0:T(8,128)(2,1)S(1)}, bf16[64,4096]{1,0:T(8,128)(2,1)S(1)}, u32[]{:S(2)}, u32[]{:S(2)}) collective-permute-start(bf16[64,4096]{1,0:T(8,128)(2,1)S(1)} %get-tuple-element.198), channel_id=1, source_target_pairs={{0,8},{8,16},{16,24},{24,32},{32,40},{40,48},{48,56},{56,64},{64,7... | collective-permute-start | bytes 1572872 | tf_op jit(solution)/shard_map/while/body/eval_jaxpr/ppermute | solution.py:11
  334.5 10.8 %collective-permute-start = (bf16[64,4096]{1,0:T(8,128)(2,1)S(1)}, bf16[64,4096]{1,0:T(8,128)(2,1)S(1)}, u32[]{:S(2)}, u32[]{:S(2)}) collective-permute-start(bf16[64,4096]{1,0:T(8,128)(2,1)S(1)} %get-tuple-element.198), channel_id=1, source_target_pairs={{0,8},{8,16},{16,24},{24,32},{32,40},{40,48},{48,56},{56,64},{64,7... | collective-permute-start | bytes 1572872 | tf_op jit(solution)/shard_map/while/body/eval_jaxpr/ppermute | solution.py:11
  348.4 10.8 %collective-permute-start = (bf16[64,4096]{1,0:T(8,128)(2,1)S(1)}, bf16[64,4096]{1,0:T(8,128)(2,1)S(1)}, u32[]{:S(2)}, u32[]{:S(2)}) collective-permute-start(bf16[64,4096]{1,0:T(8,128)(2,1)S(1)} %get-tuple-element.198), channel_id=1, source_target_pairs={{0,8},{8,16},{16,24},{24,32},{32,40},{40,48},{48,56},{56,64},{64,7... | collective-permute-start | bytes 1572872 | tf_op jit(solution)/shard_map/while/body/eval_jaxpr/ppermute | solution.py:11
  362.4 10.8 %collective-permute-start = (bf16[64,4096]{1,0:T(8,128)(2,1)S(1)}, bf16[64,4096]{1,0:T(8,128)(2,1)S(1)}, u32[]{:S(2)}, u32[]{:S(2)}) collective-permute-start(bf16[64,4096]{1,0:T(8,128)(2,1)S(1)} %get-tuple-element.198), channel_id=1, source_target_pairs={{0,8},{8,16},{16,24},{24,32},{32,40},{40,48},{48,56},{56,64},{64,7... | collective-permute-start | bytes 1572872 | tf_op jit(solution)/shard_map/while/body/eval_jaxpr/ppermute | solution.py:11
  376.3 10.8 %collective-permute-start = (bf16[64,4096]{1,0:T(8,128)(2,1)S(1)}, bf16[64,4096]{1,0:T(8,128)(2,1)S(1)}, u32[]{:S(2)}, u32[]{:S(2)}) collective-permute-start(bf16[64,4096]{1,0:T(8,128)(2,1)S(1)} %get-tuple-element.198), channel_id=1, source_target_pairs={{0,8},{8,16},{16,24},{24,32},{32,40},{40,48},{48,56},{56,64},{64,7... | collective-permute-start | bytes 1572872 | tf_op jit(solution)/shard_map/while/body/eval_jaxpr/ppermute | solution.py:11
  390.3 10.8 %collective-permute-start = (bf16[64,4096]{1,0:T(8,128)(2,1)S(1)}, bf16[64,4096]{1,0:T(8,128)(2,1)S(1)}, u32[]{:S(2)}, u32[]{:S(2)}) collective-permute-start(bf16[64,4096]{1,0:T(8,128)(2,1)S(1)} %get-tuple-element.198), channel_id=1, source_target_pairs={{0,8},{8,16},{16,24},{24,32},{32,40},{40,48},{48,56},{56,64},{64,7... | collective-permute-start | bytes 1572872 | tf_op jit(solution)/shard_map/while/body/eval_jaxpr/ppermute | solution.py:11
  404.2 10.8 %collective-permute-start = (bf16[64,4096]{1,0:T(8,128)(2,1)S(1)}, bf16[64,4096]{1,0:T(8,128)(2,1)S(1)}, u32[]{:S(2)}, u32[]{:S(2)}) collective-permute-start(bf16[64,4096]{1,0:T(8,128)(2,1)S(1)} %get-tuple-element.198), channel_id=1, source_target_pairs={{0,8},{8,16},{16,24},{24,32},{32,40},{40,48},{48,56},{56,64},{64,7... | collective-permute-start | bytes 1572872 | tf_op jit(solution)/shard_map/while/body/eval_jaxpr/ppermute | solution.py:11
  418.2 10.8 %collective-permute-start = (bf16[64,4096]{1,0:T(8,128)(2,1)S(1)}, bf16[64,4096]{1,0:T(8,128)(2,1)S(1)}, u32[]{:S(2)}, u32[]{:S(2)}) collective-permute-start(bf16[64,4096]{1,0:T(8,128)(2,1)S(1)} %get-tuple-element.198), channel_id=1, source_target_pairs={{0,8},{8,16},{16,24},{24,32},{32,40},{40,48},{48,56},{56,64},{64,7... | collective-permute-start | bytes 1572872 | tf_op jit(solution)/shard_map/while/body/eval_jaxpr/ppermute | solution.py:11
  432.1 10.8 %collective-permute-start = (bf16[64,4096]{1,0:T(8,128)(2,1)S(1)}, bf16[64,4096]{1,0:T(8,128)(2,1)S(1)}, u32[]{:S(2)}, u32[]{:S(2)}) collective-permute-start(bf16[64,4096]{1,0:T(8,128)(2,1)S(1)} %get-tuple-element.198), channel_id=1, source_target_pairs={{0,8},{8,16},{16,24},{24,32},{32,40},{40,48},{48,56},{56,64},{64,7... | collective-permute-start | bytes 1572872 | tf_op jit(solution)/shard_map/while/body/eval_jaxpr/ppermute | solution.py:11
  446.1 10.8 %collective-permute-start = (bf16[64,4096]{1,0:T(8,128)(2,1)S(1)}, bf16[64,4096]{1,0:T(8,128)(2,1)S(1)}, u32[]{:S(2)}, u32[]{:S(2)}) collective-permute-start(bf16[64,4096]{1,0:T(8,128)(2,1)S(1)} %get-tuple-element.198), channel_id=1, source_target_pairs={{0,8},{8,16},{16,24},{24,32},{32,40},{40,48},{48,56},{56,64},{64,7... | collective-permute-start | bytes 1572872 | tf_op jit(solution)/shard_map/while/body/eval_jaxpr/ppermute | solution.py:11
Sparse Core Ops, SparseCore 0:
  472.5 122.0 reduce-scatter.1
where the time goes:
time: 611 us; the launch traced here: 607 us
  waiting for transfers between devices  436 us (71%)
  matrix products  73.3 us (12%)
  local copies, waits for them, and re-layouts  60.6 us (10%)
  between operations  13.6 us (2%)
  starting transfers between devices  11.8 us (2%)
  other arithmetic  10 us (2%)
    ppermute x31, waiting for transfers between devices, shifted(): lax.ppermute(x, axis, [(i, (i + by) % length) for i in range(length)])  316 us
    reduce_scatter x1, waiting for transfers between devices, per_device(): lax.psum_scatter(partial_value, 'cd', scatter_dimension=0, tiled=True)  120 us
    dot_general x32, matrix products, contract(): jnp.einsum('isk,smk->ism', grouped, ints_sorted, preferred_element_type=j...  73.3 us
    dynamic_update_slice x32, local copies, waits for them, and re-layouts, place(): lax.dynamic_update_slice_in_dim(buffer, contract(t2_block), row_first, 0)  22.7 us
    while x1, local copies, waits for them, and re-layouts, per_device(): lax.fori_loop(1, loop_len, one_turn, (own_block, first_buf))  12.4 us
  transfers between devices with their start and end apart: 32, of which 32 were waited for; matrix products, arithmetic and copies ran while one was open for 0% of the time, Pallas kernels for 0%

commit v1 on v0

v1 whole, which is shorter than its diff:
```python
import jax
import jax.numpy as jnp
from jax import lax
from jax.experimental import pallas as pl
from jax.experimental.pallas import tpu as pltpu
from jax.sharding import PartitionSpec as P

MESH = pl.DeviceIdType.MESH
NSYM = 8
NZ = 8
NY = 4
ROWS = 64
K = 512
SLOT_K = (3, 1, 4, 2)
SLOT_BACK = (1, 0, 1, 0)
LAG2, LAG3, LAG4 = 2, 5, 7


def kernel(
    t2_ref, ints_ref, out_ref,
    gathered, weights, partial, full_hi, full_lo, half_hi, half_lo,
    xsend, xrecv, sib_send, result,
    local_sem, w_s, w_r, x0_s, x0_r, z_s, z_r, yh_s, yh_r, yf_s, yf_r, xh_s, xh_r, co_s, co_r,
):
    blk = lax.axis_index("blk")
    cd = lax.axis_index("cd")
    core = lax.rem(blk, 2)
    z = lax.rem(blk // 2, NZ)
    xl = blk // (2 * NZ)
    y = lax.rem(cd, NY)
    xh = cd // NY

    def dev(xl_, z_, core_, xh_, y_):
        return ((xl_ * NZ + z_) * 2 + core_, xh_ * NY + y_)

    def zmod(v):
        return lax.rem(v + 2 * NZ, NZ)

    def ymod(v):
        return lax.rem(v + 2 * NY, NY)

    z_dev = (dev(xl, zmod(z + 1), core, xh, y), dev(xl, zmod(z - 1), core, xh, y))
    x_dev = dev(1 - xl, z, core, xh, y)
    yp_dev = dev(xl, z, core, xh, ymod(y + 1))
    ym_dev = dev(xl, z, core, xh, ymod(y - 1))
    xh_dev = dev(xl, z, core, 1 - xh, y)
    co_dev = dev(xl, z, 1 - core, xh, y)

    def remote(src, dst, send, recv, device):
        return pltpu.make_async_remote_copy(
            src_ref=src, dst_ref=dst, send_sem=send, recv_sem=recv,
            device_id=device, device_id_type=MESH,
        )

    t2_copy = pltpu.make_async_copy(t2_ref, gathered.at[:, z, xl], local_sem.at[0])
    t2_copy.start()
    ints_copy = pltpu.make_async_copy(ints_ref, weights.at[:, pl.ds(0, 256)], local_sem.at[1])
    ints_copy.start()

    barrier = pltpu.get_barrier_semaphore()
    for device in (z_dev[0], z_dev[1], x_dev, yp_dev, ym_dev, xh_dev, co_dev):
        pl.semaphore_signal(barrier, inc=1, device_id=device, device_id_type=MESH)
    pl.semaphore_wait(barrier, 7)

    def x0_copy(s, col):
        return remote(t2_ref.at[s], gathered.at[s, z, col], x0_s.at[s], x0_r.at[s], x_dev)

    def w_copy(s):
        return remote(
            ints_ref.at[s], weights.at[s, pl.ds(256, 256)], w_s.at[s], w_r.at[s], co_dev
        )

    def send_own(s, carry):
        x0_copy(s, xl).start()
        w_copy(s).start()
        return carry

    lax.fori_loop(0, NSYM, send_own, 0)
    t2_copy.wait()
    ints_copy.wait()

    def z_copy(s, k, direction, sender_side):
        sign = -1 if direction == 0 else 1
        b = zmod(z + sign * (k - 1 if sender_side else k))
        view = gathered.at[s, b] if k < 4 else gathered.at[s, b, direction]
        return remote(view, view, z_s.at[k - 1, direction, s], z_r.at[k - 1, direction, s], z_dev[direction])

    def z_send(s, k):
        for direction in range(2):
            z_copy(s, k, direction, True).start()

    def z_recv(s, k):
        for direction in range(2):
            z_copy(s, k, direction, False).wait_recv()

    turn = jnp.where(lax.rem(z, 2) == 0, -1, 1)

    def owner(k):
        own = z // 2
        return ymod((own, own + turn, own - turn, own + 2)[k - 1])

    def half_copy(s, k, side):
        if side == 0:
            return remote(partial.at[s, k - 1, 0], half_hi.at[s], yh_s.at[0, s], yh_r.at[0, s], ym_dev)
        return remote(partial.at[s, k - 1, 1], half_lo.at[s], yh_s.at[1, s], yh_r.at[1, s], yp_dev)

    def full_copy(s, k, side):
        if side == 0:
            return remote(partial.at[s, k - 1], full_hi.at[s], yf_s.at[0, s], yf_r.at[0, s], ym_dev)
        return remote(partial.at[s, k - 1], full_lo.at[s], yf_s.at[1, s], yf_r.at[1, s], yp_dev)

    def xh_copy(s):
        return remote(xsend.at[s], xrecv.at[s], xh_s.at[s], xh_r.at[s], xh_dev)

    def co_copy(s, whose):
        return remote(
            sib_send.at[s], result.at[pl.ds(2 * s, 2), :, whose], co_s.at[s], co_r.at[s], co_dev
        )

    def stage1(s, k):
        first = 2 * owner(k)
        rows = gathered[s, pl.ds(first, 2)].reshape(4 * ROWS, K)
        product = lax.dot_general(
            rows, weights[s], (((1,), (1,)), ((), ())), preferred_element_type=jnp.float32
        )
        partial[s, k - 1] = product.astype(jnp.bfloat16).reshape(2, 2, ROWS, 512)

        @pl.when(ymod(y - owner(k)) == 2)
        def _():
            half_copy(s, k, 0).start()
            half_copy(s, k, 1).start()

    def stage2(s, k):
        d = ymod(y - owner(k))
        for side, role, recv in ((0, 1, half_hi), (1, 3, half_lo)):
            @pl.when(d == role)
            def _():
                half_copy(s, k, side).wait_recv()
                partial[s, k - 1, side] = (
                    partial[s, k - 1, side].astype(jnp.float32) + recv[s].astype(jnp.float32)
                ).astype(jnp.bfloat16)
                full_copy(s, k, side).start()

    def three(s, k, col):
        return (
            partial[s, k - 1, :, col].astype(jnp.float32)
            + full_hi[s, :, col].astype(jnp.float32)
            + full_lo[s, :, col].astype(jnp.float32)
        )

    def stage3(s, k):
        @pl.when(y == owner(k))
        def _():
            full_copy(s, k, 0).wait_recv()
            full_copy(s, k, 1).wait_recv()
            xsend[s] = three(s, k, 1 - xh).astype(jnp.bfloat16)
            xh_copy(s).start()

    def stage4(s, k):
        @pl.when(y == owner(k))
        def _():
            xh_copy(s).wait_recv()
            final = (three(s, k, xh) + xrecv[s].astype(jnp.float32)).astype(jnp.bfloat16)
            for h in range(2):
                result[2 * s + h, :, core] = final[:, :, 128 * h:128 * (h + 1)]
                sib_send[s, h] = final[:, :, 256 + 128 * h:256 + 128 * (h + 1)]
            co_copy(s, core).start()

    def when_valid(s, act):
        @pl.when(jnp.logical_and(s >= 0, s < NSYM))
        def _():
            act()

    def lagged(tick, slot, lag, stage):
        q = slot - lag
        j, back = q % 4, q // 4
        s = tick + back - SLOT_BACK[j]
        when_valid(s, lambda: stage(s, SLOT_K[j]))

    def tick_body(tick, carry):
        def begin():
            x0_copy(tick, 1 - xl).wait_recv()
            z_send(tick, 1)

        when_valid(tick, begin)
        for slot in range(4):
            k, s = SLOT_K[slot], tick - SLOT_BACK[slot]

            def arrive(k=k, s=s):
                z_recv(s, k)
                if k < 4:
                    z_send(s, k + 1)
                if k == 1:
                    w_copy(s).wait_recv()
                stage1(s, k)

            when_valid(s, arrive)
            lagged(tick, slot, LAG2, stage2)
            lagged(tick, slot, LAG3, stage3)
            lagged(tick, slot, LAG4, stage4)
        return carry

    lax.fori_loop(0, NSYM + 1 + (LAG4 + 3) // 4, tick_body, 0)

    def drain(s, carry):
        x0_copy(s, xl).wait_send()
        w_copy(s).wait_send()
        for k in range(1, 5):
            for direction in range(2):
                z_copy(s, k, direction, True).wait_send()
        for side in range(2):
            half_copy(s, 1, side).wait_send()
            full_copy(s, 1, side).wait_send()
        xh_copy(s).wait_send()
        co_copy(s, core).wait_send()
        co_copy(s, 1 - core).wait_recv()
        return carry

    lax.fori_loop(0, NSYM, drain, 0)

    out_copy = pltpu.make_async_copy(result, out_ref, local_sem.at[0])
    out_copy.start()
    out_copy.wait()


def merge_tiles(load, first, second):
    pieces = []
    for want, tile in ((0, first), (1, second)):
        a = load(tile // 2).astype(jnp.float32)
        pieces.append(jnp.where(lax.rem(tile, 2) == want, a, pltpu.roll(a, 64, 1)))
    lane = lax.broadcasted_iota(jnp.int32, pieces[0].shape, 1)
    return jnp.where(lane < 64, pieces[0], pieces[1]).astype(jnp.bfloat16)


def sort_kernel(ab_ref, cd_ref, t2_ref, ints_ref, t2_out, ints_out, inverse_ref, order, count):
    def clear(s, carry):
        count[s] = 0
        count[NSYM + s] = 0
        return carry

    lax.fori_loop(0, NSYM, clear, 0)

    def place_cd(i, carry):
        s = cd_ref[i]
        c = count[s]
        order[s * 8 + c] = i
        count[s] = c + 1
        return carry

    lax.fori_loop(0, 64, place_cd, 0)

    def place_ab(i, carry):
        s = ab_ref[i]
        c = count[NSYM + s]
        inverse_ref[i] = s * 4 + c
        ints_out[s, pl.ds(pl.multiple_of(c * 64, 64), 64)] = ints_ref[i]
        count[NSYM + s] = c + 1
        return carry

    lax.fori_loop(0, 32, place_ab, 0)

    def load(chunk):
        return t2_ref[:, pl.ds(pl.multiple_of(chunk * 128, 128), 128)]

    def sort_t2(s, carry):
        for j in range(K // 128):
            t2_out[s, :, 128 * j:128 * (j + 1)] = merge_tiles(
                load, order[s * 8 + 2 * j], order[s * 8 + 2 * j + 1]
            )
        return carry

    lax.fori_loop(0, NSYM, sort_t2, 0)


def unsort_kernel(inverse_ref, sorted_ref, out_ref):
    for p in range(16):
        out_ref[:, 128 * p:128 * (p + 1)] = merge_tiles(
            lambda chunk: sorted_ref[chunk], inverse_ref[2 * p], inverse_ref[2 * p + 1]
        )


def per_device(t2_amps, integrals, ab_sym, cd_sym):
    bf16 = jnp.bfloat16
    dma = pltpu.SemaphoreType.DMA
    smem = pl.BlockSpec(memory_space=pltpu.SMEM)
    vmem = pl.BlockSpec(memory_space=pltpu.VMEM)
    t2_sorted, ints_sorted, inverse = pl.pallas_call(
        sort_kernel,
        out_shape=(
            jax.ShapeDtypeStruct((NSYM, ROWS, K), bf16),
            jax.ShapeDtypeStruct((NSYM, 256, K), bf16),
            jax.ShapeDtypeStruct((32,), jnp.int32),
        ),
        in_specs=[smem, smem, vmem, vmem],
        out_specs=(vmem, vmem, smem),
        scratch_shapes=[pltpu.SMEM((64,), jnp.int32), pltpu.SMEM((16,), jnp.int32)],
    )(ab_sym, cd_sym, t2_amps, integrals)
    result = pl.pallas_call(
        kernel,
        out_shape=jax.ShapeDtypeStruct((2 * NSYM, 2, 2, ROWS, 128), bf16),
        in_specs=[
            pl.BlockSpec(memory_space=pl.ANY),
            pl.BlockSpec(memory_space=pl.ANY),
        ],
        out_specs=pl.BlockSpec(memory_space=pl.ANY),
        scratch_shapes=[
            pltpu.VMEM((NSYM, NZ, 2, ROWS, K), bf16),
            pltpu.VMEM((NSYM, 512, K), bf16),
            pltpu.VMEM((NSYM, 4, 2, 2, ROWS, 512), bf16),
            pltpu.VMEM((NSYM, 2, 2, ROWS, 512), bf16),
            pltpu.VMEM((NSYM, 2, 2, ROWS, 512), bf16),
            pltpu.VMEM((NSYM, 2, ROWS, 512), bf16),
            pltpu.VMEM((NSYM, 2, ROWS, 512), bf16),
            pltpu.VMEM((NSYM, 2, ROWS, 512), bf16),
            pltpu.VMEM((NSYM, 2, ROWS, 512), bf16),
            pltpu.VMEM((NSYM, 2, 2, ROWS, 128), bf16),
            pltpu.VMEM((2 * NSYM, 2, 2, ROWS, 128), bf16),
            dma((2,)),
            dma((NSYM,)), dma((NSYM,)),
            dma((NSYM,)), dma((NSYM,)),
            dma((4, 2, NSYM)), dma((4, 2, NSYM)),
            dma((2, NSYM)), dma((2, NSYM)),
            dma((2, NSYM)), dma((2, NSYM)),
            dma((NSYM,)), dma((NSYM,)),
            dma((NSYM,)), dma((NSYM,)),
        ],
        compiler_params=pltpu.CompilerParams(
            collective_id=0, has_side_effects=True, vmem_limit_bytes=40 << 20
        ),
    )(t2_sorted, ints_sorted)
    return pl.pallas_call(
        unsort_kernel,
        out_shape=jax.ShapeDtypeStruct((256, 2048), bf16),
        in_specs=[smem, vmem],
        out_specs=vmem,
    )(inverse, result.reshape(2 * NSYM, 256, 128))


def solution(mesh):
    in_specs = (P("blk", "cd"), P("blk", None, "cd"), P("blk"), P("cd"))
    out_specs = P("cd", "blk")
    return jax.shard_map(
        per_device, mesh=mesh, in_specs=in_specs, out_specs=out_specs, check_vma=False
    )
```

time: 611 us -> 152 us (0.25)
  waiting for transfers between devices: 436 us -> 0 us
  Pallas kernels: 0 us -> 148 us
  matrix products: 73.3 us -> 0 us
  local copies, waits for them, and re-layouts: 60.6 us -> 3.59 us
  between operations: 13.6 us -> 0.03 us
  starting transfers between devices: 11.8 us -> 0 us
  other arithmetic: 10 us -> 0 us
    ppermute x31 -> x0, waiting for transfers between devices: 316 us -> none  [shifted(): lax.ppermute(x, axis, [(i, (i + by) % length) for i in range(length)])]
    pallas_call x0 -> x3, Pallas kernels: none -> 148 us  [the longest x1 139 us: per_device(): pl.pallas_call(kernel, out_shape=jax.ShapeDtypeStruct((2 * NSYM, 2, 2, RO...]
    reduce_scatter x1 -> x0, waiting for transfers between devices: 120 us -> none  [per_device(): lax.psum_scatter(partial_value, 'cd', scatter_dimension=0, tiled=True)]
    dot_general x32 -> x0, matrix products: 73.3 us -> none  [contract(): jnp.einsum('isk,smk->ism', grouped, ints_sorted, preferred_element_type=j...]
    dynamic_update_slice x32 -> x0, local copies, waits for them, and re-layouts: 22.7 us -> none  [place(): lax.dynamic_update_slice_in_dim(buffer, contract(t2_block), row_first, 0)]
    while x32 -> x0, local copies, waits for them, and re-layouts: 13.4 us -> none  [the longest x1 12.4 us: per_device(): lax.fori_loop(1, loop_len, one_turn, (own_block, first_buf))]
    ppermute x31 -> x0, starting transfers between devices: 11.8 us -> none  [shifted(): lax.ppermute(x, axis, [(i, (i + by) % length) for i in range(length)])]
    gather x6 -> x0, local copies, waits for them, and re-layouts: 10.4 us -> none  [the longest x4 6.57 us: per_device(): jnp.take(t2_amps.reshape(block_rows, cd_tiles, tile_width), order_cd, axi...]
  transfers between devices with their start and end apart: 32 -> 0, of which waited for: 32 -> 0; matrix products, arithmetic and copies ran while one was open for 0% -> 0% of each run, Pallas kernels for 0% -> 0%
where the time goes in v1:
time: 152 us; the launch traced here: 151 us
  Pallas kernels  148 us (97%)
  local copies, waits for them, and re-layouts  3.59 us (2%)
    pallas_call x1, Pallas kernels, per_device(): pl.pallas_call(kernel, out_shape=jax.ShapeDtypeStruct((2 * NSYM, 2, 2, RO...  139 us
    pallas_call x1, Pallas kernels, per_device(): pl.pallas_call(sort_kernel, out_shape=(jax.ShapeDtypeStruct((NSYM, ROWS,...  5.56 us
    unnamed x6, local copies, waits for them, and re-layouts  3.59 us
    pallas_call x1, Pallas kernels, per_device(): pl.pallas_call(unsort_kernel, out_shape=jax.ShapeDtypeStruct((256, 2048),...  3.07 us

profile of v1, /device:TPU:17, one launch (start us, length us, event | category | flops | bytes accessed | tf_op | source)
XLA Modules:
  0.0 151.4 jit_solution(5412034274968670800)
XLA Ops:
  0.0 5.6 %shard_map.46 = (bf16[8,64,512]{2,1,0:T(8,128)(2,1)}, bf16[8,256,512]{2,1,0:T(8,128)(2,1)}, s32[32]{0:T(128)}) custom-call(s32[32]{0:T(128)} %ab_ref.1, s32[64]{0:T(128)} %cd_ref.1, bf16[64,4096]{1,0:T(8,128)(2,1)} %t2_ref.1, bf16[32,64,512]{2,1,0:T(8,128)(2,1)} %ints_ref.1), custom_call_target="tpu_custom_call" | custom-call | tf_op jit(solution)/shard_map/pallas_call | solution.py:287
  5.6 0.0 copy-start.1
  5.6 1.6 %copy-done.1 = bf16[8,256,512]{2,1,0:T(8,128)(2,1)S(1)} copy-done((bf16[8,256,512]{2,1,0:T(8,128)(2,1)S(1)}, bf16[8,256,512]{2,1,0:T(8,128)(2,1)}, u32[]{:S(2)}) %copy-start.1) | copy-done | bytes 2097176
  7.2 0.0 copy-start.2
  7.2 1.0 copy-done.2
  8.2 139.1 %shard_map.47 = bf16[16,2,2,64,128]{4,3,2,1,0:T(8,128)(2,1)S(1)} custom-call(bf16[8,64,512]{2,1,0:T(8,128)(2,1)S(1)} %copy-done.2, bf16[8,256,512]{2,1,0:T(8,128)(2,1)S(1)} %copy-done.1), custom_call_target="tpu_custom_call" | custom-call | tf_op jit(solution)/shard_map/pallas_call | solution.py:298
  147.3 0.0 copy-start
  147.3 1.0 copy-done
  148.3 3.1 %shard_map.48 = bf16[256,2048]{1,0:T(8,128)(2,1)} custom-call(s32[32]{0:T(128)} %get-tuple-element.8.inverse_ref, bf16[16,256,128]{2,1,0:T(8,128)(2,1)} %bitcast.1), custom_call_target="tpu_custom_call" | custom-call | tf_op jit(solution)/shard_map/pallas_call | solution.py:331
Async XLA Ops:
  5.6 1.6 %copy-start.1 = (bf16[8,256,512]{2,1,0:T(8,128)(2,1)S(1)}, bf16[8,256,512]{2,1,0:T(8,128)(2,1)}, u32[]{:S(2)}) copy-start(bf16[8,256,512]{2,1,0:T(8,128)(2,1)} %get-tuple-element.10.ints_ref) | copy-start | bytes 6291460
  7.2 1.0 copy-start.2
  147.3 1.0 copy-start

commit v2 on v1

--- a/solution.py
+++ b/solution.py
@@ -11,16 +11,16 @@
 NY = 4
 ROWS = 64
 K = 512
-SLOT_K = (3, 1, 4, 2)
-SLOT_BACK = (1, 0, 1, 0)
-LAG2, LAG3, LAG4 = 2, 5, 7
+SLOT_K = (2, 3, 1, 4)
+SLOT_BACK = (1, 2, 0, 2)
+LAG2, LAG3, LAG4 = 3, 7, 10
 
 
 def kernel(
     t2_ref, ints_ref, out_ref,
     gathered, weights, partial, full_hi, full_lo, half_hi, half_lo,
     xsend, xrecv, sib_send, result,
-    local_sem, w_s, w_r, x0_s, x0_r, z_s, z_r, yh_s, yh_r, yf_s, yf_r, xh_s, xh_r, co_s, co_r,
+    local_sem, w_s, w_r, x0_s, x0_r, z_s, z_r, xf_s, xf_r, yh_s, yh_r, yf_s, yf_r, xh_s, xh_r, co_s, co_r,
 ):
     blk = lax.axis_index("blk")
     cd = lax.axis_index("cd")
@@ -82,7 +82,12 @@
     def z_copy(s, k, direction, sender_side):
         sign = -1 if direction == 0 else 1
         b = zmod(z + sign * (k - 1 if sender_side else k))
-        view = gathered.at[s, b] if k < 4 else gathered.at[s, b, direction]
+        if k < 3:
+            view = gathered.at[s, b]
+        elif k == 3:
+            view = gathered.at[s, b, xl]
+        else:
+            view = gathered.at[s, b, xl, pl.ds(32 * direction, 32)]
         return remote(view, view, z_s.at[k - 1, direction, s], z_r.at[k - 1, direction, s], z_dev[direction])
 
     def z_send(s, k):
@@ -92,6 +97,11 @@
     def z_recv(s, k):
         for direction in range(2):
             z_copy(s, k, direction, False).wait_recv()
+
+    def xf_copy(s, f, sender_side):
+        col = xl if sender_side else 1 - xl
+        view = gathered.at[s, zmod(z + (-3, 3, 4)[f]), col]
+        return remote(view, view, xf_s.at[f, s], xf_r.at[f, s], x_dev)
 
     turn = jnp.where(lax.rem(z, 2) == 0, -1, 1)
 
@@ -177,30 +187,52 @@
         s = tick + back - SLOT_BACK[j]
         when_valid(s, lambda: stage(s, SLOT_K[j]))
 
+    def begin(s):
+        x0_copy(s, 1 - xl).wait_recv()
+        z_send(s, 1)
+
+    def arrive(s, k):
+        z_recv(s, k)
+        if k < 4:
+            z_send(s, k + 1)
+        if k == 3:
+            xf_copy(s, 0, True).start()
+            xf_copy(s, 1, True).start()
+        if k == 4:
+            xf_copy(s, 2, True).start()
+
+    def multiply(s, k):
+        if k == 1:
+            w_copy(s).wait_recv()
+        if k == 3:
+            xf_copy(s, 0, False).wait_recv()
+            xf_copy(s, 1, False).wait_recv()
+        if k == 4:
+            xf_copy(s, 2, False).wait_recv()
+        stage1(s, k)
+
     def tick_body(tick, carry):
-        def begin():
-            x0_copy(tick, 1 - xl).wait_recv()
-            z_send(tick, 1)
-
-        when_valid(tick, begin)
-        for slot in range(4):
-            k, s = SLOT_K[slot], tick - SLOT_BACK[slot]
-
-            def arrive(k=k, s=s):
-                z_recv(s, k)
-                if k < 4:
-                    z_send(s, k + 1)
-                if k == 1:
-                    w_copy(s).wait_recv()
-                stage1(s, k)
-
-            when_valid(s, arrive)
+        def run(back, act, *args):
+            when_valid(tick - back, lambda: act(tick - back, *args))
+
+        def unit(slot):
+            run(SLOT_BACK[slot], multiply, SLOT_K[slot])
             lagged(tick, slot, LAG2, stage2)
             lagged(tick, slot, LAG3, stage3)
             lagged(tick, slot, LAG4, stage4)
-        return carry
-
-    lax.fori_loop(0, NSYM + 1 + (LAG4 + 3) // 4, tick_body, 0)
+
+        run(0, begin)
+        run(2, arrive, 4)
+        run(1, arrive, 2)
+        unit(0)
+        unit(1)
+        run(0, arrive, 1)
+        unit(2)
+        run(1, arrive, 3)
+        unit(3)
+        return carry
+
+    lax.fori_loop(0, NSYM + 2 + (LAG4 + 3) // 4, tick_body, 0)
 
     def drain(s, carry):
         x0_copy(s, xl).wait_send()
@@ -208,6 +240,8 @@
         for k in range(1, 5):
             for direction in range(2):
                 z_copy(s, k, direction, True).wait_send()
+        for f in range(3):
+            xf_copy(s, f, True).wait_send()
         for side in range(2):
             half_copy(s, 1, side).wait_send()
             full_copy(s, 1, side).wait_send()
@@ -226,13 +260,13 @@
 def merge_tiles(load, first, second):
     pieces = []
     for want, tile in ((0, first), (1, second)):
-        a = load(tile // 2).astype(jnp.float32)
+        a = load(tile // 2)
         pieces.append(jnp.where(lax.rem(tile, 2) == want, a, pltpu.roll(a, 64, 1)))
     lane = lax.broadcasted_iota(jnp.int32, pieces[0].shape, 1)
-    return jnp.where(lane < 64, pieces[0], pieces[1]).astype(jnp.bfloat16)
-
-
-def sort_kernel(ab_ref, cd_ref, t2_ref, ints_ref, t2_out, ints_out, inverse_ref, order, count):
+    return jnp.where(lane < 64, pieces[0], pieces[1])
+
+
+def sort_kernel(ab_ref, cd_ref, t2_ref, ints_ref, t2_out, ints_out, inverse_ref, order, count, sem):
     def clear(s, carry):
         count[s] = 0
         count[NSYM + s] = 0
@@ -253,11 +287,12 @@
         s = ab_ref[i]
         c = count[NSYM + s]
         inverse_ref[i] = s * 4 + c
-        ints_out[s, pl.ds(pl.multiple_of(c * 64, 64), 64)] = ints_ref[i]
+        pltpu.make_async_copy(ints_ref.at[i], ints_out.at[s, c], sem).start()
         count[NSYM + s] = c + 1
         return carry
 
     lax.fori_loop(0, 32, place_ab, 0)
+    whole = pltpu.make_async_copy(ints_out, ints_out, sem)
 
     def load(chunk):
         return t2_ref[:, pl.ds(pl.multiple_of(chunk * 128, 128), 128)]
@@ -270,6 +305,7 @@
         return carry
 
     lax.fori_loop(0, NSYM, sort_t2, 0)
+    whole.wait()
 
 
 def unsort_kernel(inverse_ref, sorted_ref, out_ref):
@@ -284,25 +320,23 @@
     dma = pltpu.SemaphoreType.DMA
     smem = pl.BlockSpec(memory_space=pltpu.SMEM)
     vmem = pl.BlockSpec(memory_space=pltpu.VMEM)
+    hbm = pl.BlockSpec(memory_space=pltpu.HBM)
     t2_sorted, ints_sorted, inverse = pl.pallas_call(
         sort_kernel,
         out_shape=(
             jax.ShapeDtypeStruct((NSYM, ROWS, K), bf16),
-            jax.ShapeDtypeStruct((NSYM, 256, K), bf16),
+            jax.ShapeDtypeStruct((NSYM, 4, 64, K), bf16),
             jax.ShapeDtypeStruct((32,), jnp.int32),
         ),
-        in_specs=[smem, smem, vmem, vmem],
+        in_specs=[smem, smem, vmem, hbm],
         out_specs=(vmem, vmem, smem),
-        scratch_shapes=[pltpu.SMEM((64,), jnp.int32), pltpu.SMEM((16,), jnp.int32)],
+        scratch_shapes=[pltpu.SMEM((64,), jnp.int32), pltpu.SMEM((16,), jnp.int32), dma(())],
     )(ab_sym, cd_sym, t2_amps, integrals)
     result = pl.pallas_call(
         kernel,
         out_shape=jax.ShapeDtypeStruct((2 * NSYM, 2, 2, ROWS, 128), bf16),
-        in_specs=[
-            pl.BlockSpec(memory_space=pl.ANY),
-            pl.BlockSpec(memory_space=pl.ANY),
-        ],
-        out_specs=pl.BlockSpec(memory_space=pl.ANY),
+        in_specs=[hbm, hbm],
+        out_specs=hbm,
         scratch_shapes=[
             pltpu.VMEM((NSYM, NZ, 2, ROWS, K), bf16),
             pltpu.VMEM((NSYM, 512, K), bf16),
@@ -319,20 +353,22 @@
             dma((NSYM,)), dma((NSYM,)),
             dma((NSYM,)), dma((NSYM,)),
             dma((4, 2, NSYM)), dma((4, 2, NSYM)),
+            dma((3, NSYM)), dma((3, NSYM)),
             dma((2, NSYM)), dma((2, NSYM)),
             dma((2, NSYM)), dma((2, NSYM)),
             dma((NSYM,)), dma((NSYM,)),
             dma((NSYM,)), dma((NSYM,)),
         ],
         compiler_params=pltpu.CompilerParams(
-            collective_id=0, has_side_effects=True, vmem_limit_bytes=40 << 20
+            collective_id=0, has_side_effects=True, vmem_limit_bytes=62 << 20
         ),
-    )(t2_sorted, ints_sorted)
+    )(t2_sorted, ints_sorted.reshape(NSYM, 256, K))
     return pl.pallas_call(
         unsort_kernel,
         out_shape=jax.ShapeDtypeStruct((256, 2048), bf16),
-        in_specs=[smem, vmem],
-        out_specs=vmem,
+        grid=(4,),
+        in_specs=[smem, pl.BlockSpec((2 * NSYM, ROWS, 128), lambda i: (0, i, 0))],
+        out_specs=pl.BlockSpec((ROWS, 2048), lambda i: (i, 0)),
     )(inverse, result.reshape(2 * NSYM, 256, 128))
 
 

time: 152 us -> 128 us (0.84)
  Pallas kernels: 148 us -> 127 us
  local copies, waits for them, and re-layouts: 3.59 us -> 0 us
    pallas_call x1, Pallas kernels: 139 us -> 118 us  [per_device(): pl.pallas_call(kernel, out_shape=jax.ShapeDtypeStruct((2 * NSYM, 2, 2, RO...]
    unnamed x6 -> x0, local copies, waits for them, and re-layouts: 3.59 us -> none
where the time goes in v2:
time: 128 us
  Pallas kernels  127 us (99%)
    pallas_call x1, Pallas kernels, per_device(): pl.pallas_call(kernel, out_shape=jax.ShapeDtypeStruct((2 * NSYM, 2, 2, RO...  118 us
    pallas_call x1, Pallas kernels, per_device(): pl.pallas_call(sort_kernel, out_shape=(jax.ShapeDtypeStruct((NSYM, ROWS,...  5.1 us
    pallas_call x1, Pallas kernels, per_device(): pl.pallas_call(unsort_kernel, out_shape=jax.ShapeDtypeStruct((256, 2048),...  3.96 us

profile of v2, /device:TPU:17, one launch (start us, length us, event | category | flops | bytes accessed | tf_op | source)
XLA Modules:
  0.0 127.5 jit_solution(5206254922556946426)
XLA Ops:
  0.0 5.1 %shard_map.46 = (bf16[8,64,512]{2,1,0:T(8,128)(2,1)}, bf16[8,4,64,512]{3,2,1,0:T(8,128)(2,1)}, s32[32]{0:T(128)}) custom-call(s32[32]{0:T(128)} %ab_ref.1, s32[64]{0:T(128)} %cd_ref.1, bf16[64,4096]{1,0:T(8,128)(2,1)} %t2_ref.1, bf16[32,64,512]{2,1,0:T(8,128)(2,1)} %ints_ref.1), custom_call_target="tpu_custom_call" | custom-call | tf_op jit(solution)/shard_map/pallas_call | solution.py:324
  5.1 118.4 %shard_map.47 = bf16[16,2,2,64,128]{4,3,2,1,0:T(8,128)(2,1)} custom-call(bf16[8,64,512]{2,1,0:T(8,128)(2,1)} %get-tuple-element.9.t2_ref, bf16[8,256,512]{2,1,0:T(8,128)(2,1)} %bitcast.3), custom_call_target="tpu_custom_call" | custom-call | tf_op jit(solution)/shard_map/pallas_call | solution.py:335
  123.5 4.0 %shard_map.48 = bf16[256,2048]{1,0:T(8,128)(2,1)} custom-call(s32[32]{0:T(128)} %get-tuple-element.8.inverse_ref, bf16[16,256,128]{2,1,0:T(8,128)(2,1)} %bitcast.2), custom_call_target="tpu_custom_call" | custom-call | tf_op jit(solution)/shard_map/pallas_call | solution.py:366

commit v3 on v2

v3 whole, which is shorter than its diff:
```python
import jax
import jax.numpy as jnp
from jax import lax
from jax.experimental import pallas as pl
from jax.experimental.pallas import tpu as pltpu
from jax.sharding import PartitionSpec as P

MESH = pl.DeviceIdType.MESH
NSYM = 8
NZ = 8
NY = 4
ROWS = 64
K = 512
WIDE = 6
NARROW = NSYM - WIDE
EARLY = 2
SCHEDULE = (
    ("begin", 0, 0),
    ("add", 3, 3),
    ("arrive", 2, 1),
    ("arrive", 4, 2),
    ("multiply", 3, 2),
    ("add", 2, 2),
    ("multiply", 2, 1),
    ("finish", 3, 5),
    ("own", 3, 4),
    ("finish", 2, 4),
    ("own", 2, 3),
    ("forward", 0, -2),
    ("arrive", 1, 0),
    ("rows", 0, -6),
    ("add", 1, 1),
    ("add", 4, 3),
    ("arrive", 3, 1),
    ("multiply", 1, 0),
    ("multiply", 4, 2),
    ("weights", 0, -6),
    ("finish", 1, 3),
    ("finish", 4, 5),
    ("own", 1, 2),
    ("own", 4, 4),
    ("first", 1, -2),
)


def kernel(
    t2_ref, ints_ref, out_ref,
    gathered, weights, partial, full_hi, full_lo, half_hi, half_lo, xsend, xrecv,
    n_partial, n_full_hi, n_full_lo, n_half_hi, n_half_lo, n_sib, sib_send, result,
    local_sem, w_s, w_r, x0_s, x0_r, z_s, z_r, xf_s, xf_r, yh_s, yh_r, yf_s, yf_r, xh_s, xh_r,
    co_s, co_r, wx_s, wx_r, wf_s, wf_r, pb_s, pb_r,
):
    blk = lax.axis_index("blk")
    cd = lax.axis_index("cd")
    core = lax.rem(blk, 2)
    z = lax.rem(blk // 2, NZ)
    xl = blk // (2 * NZ)
    y = lax.rem(cd, NY)
    xh = cd // NY

    def dev(xl_, z_, core_, xh_, y_):
        return ((xl_ * NZ + z_) * 2 + core_, xh_ * NY + y_)

    def zmod(v):
        return lax.rem(v + 2 * NZ, NZ)

    def ymod(v):
        return lax.rem(v + 2 * NY, NY)

    z_dev = (dev(xl, zmod(z + 1), core, xh, y), dev(xl, zmod(z - 1), core, xh, y))
    x_dev = dev(1 - xl, z, core, xh, y)
    xh_dev = dev(xl, z, core, 1 - xh, y)
    xd_dev = dev(1 - xl, z, core, 1 - xh, y)
    yp_dev = dev(xl, z, core, xh, ymod(y + 1))
    ym_dev = dev(xl, z, core, xh, ymod(y - 1))
    co_dev = dev(xl, z, 1 - core, xh, y)
    yp_other = dev(xl, z, 1 - core, xh, ymod(y + 1))
    ym_other = dev(xl, z, 1 - core, xh, ymod(y - 1))
    outer = xl == xh
    inner = jnp.logical_not(outer)
    wide, narrow = pl.ds(0, WIDE), pl.ds(WIDE, NARROW)

    def remote(src, dst, send, recv, device):
        return pltpu.make_async_remote_copy(
            src_ref=src, dst_ref=dst, send_sem=send, recv_sem=recv,
            device_id=device, device_id_type=MESH,
        )

    ints_copy = pltpu.make_async_copy(ints_ref, weights.at[:, xh, pl.ds(0, 256)], local_sem.at[0])
    ints_copy.start()
    t2_copy = pltpu.make_async_copy(t2_ref.at[wide], gathered.at[wide, z, xl], local_sem.at[1])
    t2_copy.start()
    t2_narrow = pltpu.make_async_copy(
        t2_ref.at[narrow], gathered.at[narrow, z, xh], local_sem.at[2]
    )

    @pl.when(outer)
    def _():
        t2_narrow.start()

    barrier = pltpu.get_barrier_semaphore()
    for device in (
        z_dev[0], z_dev[1], x_dev, xh_dev, xd_dev, yp_dev, ym_dev, co_dev, yp_other, ym_other
    ):
        pl.semaphore_signal(barrier, inc=1, device_id=device, device_id_type=MESH)
    pl.semaphore_wait(barrier, 10)

    def x0_copy(s, col):
        return remote(t2_ref.at[s], gathered.at[s, z, col], x0_s.at[s], x0_r.at[s], x_dev)

    def pb_copy(s, i, group):
        return remote(
            t2_ref.at[s], gathered.at[s, z, group], pb_s.at[i, s], pb_r.at[s], (xd_dev, xh_dev)[i]
        )

    def send_rows(s, k):
        @pl.when(outer)
        def _():
            x0_copy(s, xh).start()

        @pl.when(inner)
        def _():
            pb_copy(s, 0, xh).start()
            pb_copy(s, 1, xh).start()

    def w_copy(s):
        return remote(
            ints_ref.at[s], weights.at[s, xh, pl.ds(256, 256)], w_s.at[s], w_r.at[s], co_dev
        )

    def wx_copy(s, group):
        return remote(
            ints_ref.at[s], weights.at[s, group, pl.ds(0, 256)], wx_s.at[s], wx_r.at[s], xh_dev
        )

    def wf_copy(s):
        return remote(
            weights.at[s, 1 - xh, pl.ds(0, 256)], weights.at[s, 1 - xh, pl.ds(256, 256)],
            wf_s.at[s], wf_r.at[s], co_dev,
        )

    def send_weights(s, k):
        wx_copy(s, xh).start()

    def forward_weights(s, k):
        wx_copy(s, 1 - xh).wait_recv()
        wf_copy(s).start()

    def z_copy(s, k, direction, sender_side, is_wide):
        sign = -1 if direction == 0 else 1
        b = zmod(z + sign * (k - 1 if sender_side else k))
        if k < 3 or (k == 3 and not is_wide):
            view = gathered.at[s, b]
        elif k == 3:
            view = gathered.at[s, b, xl]
        elif is_wide:
            view = gathered.at[s, b, xl, pl.ds(32 * direction, 32)]
        else:
            view = gathered.at[s, b, direction]
        return remote(view, view, z_s.at[k - 1, direction, s], z_r.at[k - 1, direction, s], z_dev[direction])

    def z_one(s, direction, sender_side, own):
        b = z if sender_side else zmod(z + (-1 if direction == 0 else 1))
        view = gathered.at[s, b, xl if own else 1 - xl]
        i = 0 if own else 4
        return remote(view, view, z_s.at[i, direction, s], z_r.at[i, direction, s], z_dev[direction])

    def z_send(s, k, is_wide):
        for direction in range(2):
            z_copy(s, k, direction, True, is_wide).start()

    def z_recv(s, k, is_wide):
        for direction in range(2):
            if is_wide and k == 1:
                z_one(s, direction, False, True).wait_recv()
                z_one(s, direction, False, False).wait_recv()
            else:
                z_copy(s, k, direction, False, is_wide).wait_recv()

    def xf_copy(s, f, sender_side):
        col = xl if sender_side else 1 - xl
        view = gathered.at[s, zmod(z + (-3, 3, 4)[f]), col]
        return remote(view, view, xf_s.at[f, s], xf_r.at[f, s], x_dev)

    turn = jnp.where(lax.rem(z, 2) == 0, -1, 1)

    def owner(k):
        own = z // 2
        return ymod((own, own + turn, own - turn, own + 2)[k - 1])

    def buffers(is_wide, s):
        if is_wide:
            return s, partial, full_hi, full_lo, half_hi, half_lo
        return s - WIDE, n_partial, n_full_hi, n_full_lo, n_half_hi, n_half_lo

    def half_copy(s, k, side, is_wide):
        i, part, _, _, hi, lo = buffers(is_wide, s)
        return remote(
            part.at[i, k - 1, side], (hi, lo)[side].at[i], yh_s.at[side, s], yh_r.at[side, s],
            (ym_dev, yp_dev)[side],
        )

    def full_copy(s, k, side, is_wide):
        i, part, hi, lo, _, _ = buffers(is_wide, s)
        return remote(
            part.at[i, k - 1], (hi, lo)[side].at[i], yf_s.at[side, s], yf_r.at[side, s],
            (ym_dev, yp_dev)[side],
        )

    def n_full_copy(s, k, side, other):
        return remote(
            n_partial.at[s - WIDE, k - 1, :, :, pl.ds(256 * other, 256)],
            (n_full_hi, n_full_lo)[side].at[s - WIDE, other],
            yf_s.at[side + 2 * other, s], yf_r.at[side + 2 * other, s],
            ((ym_dev, yp_dev), (ym_other, yp_other))[other][side],
        )

    def n_sib_copy(s, k):
        return remote(
            n_partial.at[s - WIDE, k - 1, :, :, pl.ds(256, 256)], n_sib.at[s - WIDE],
            co_s.at[s], co_r.at[s], co_dev,
        )

    def xh_copy(s):
        return remote(xsend.at[s], xrecv.at[s], xh_s.at[s], xh_r.at[s], xh_dev)

    def co_copy(s, whose):
        return remote(
            sib_send.at[s], result.at[pl.ds(2 * s, 2), :, whose], co_s.at[s], co_r.at[s], co_dev
        )

    def contract(rows, w):
        return lax.dot_general(rows, w, (((1,), (1,)), ((), ())), preferred_element_type=jnp.float32)

    def stage1(s, k, is_wide):
        first = pl.ds(2 * owner(k), 2)
        i, part = buffers(is_wide, s)[:2]
        if is_wide:
            product = contract(gathered[s, first].reshape(4 * ROWS, K), weights[s, xh])
            part[i, k - 1] = product.astype(jnp.bfloat16).reshape(2, 2, ROWS, 512)
        else:
            product = contract(
                gathered[s, first, 0].reshape(2 * ROWS, K), weights[s, 0]
            ) + contract(gathered[s, first, 1].reshape(2 * ROWS, K), weights[s, 1])
            part[i, k - 1] = product.astype(jnp.bfloat16).reshape(2, ROWS, 512)

            @pl.when(y == owner(k))
            def _():
                n_sib_copy(s, k).start()

        @pl.when(ymod(y - owner(k)) == 2)
        def _():
            half_copy(s, k, 0, is_wide).start()
            half_copy(s, k, 1, is_wide).start()

    def stage2(s, k, is_wide):
        i, part, _, _, hi, lo = buffers(is_wide, s)
        d = ymod(y - owner(k))
        for side, role, recv in ((0, 1, hi), (1, 3, lo)):
            @pl.when(d == role)
            def _():
                half_copy(s, k, side, is_wide).wait_recv()
                part[i, k - 1, side] = (
                    part[i, k - 1, side].astype(jnp.float32) + recv[i].astype(jnp.float32)
                ).astype(jnp.bfloat16)
                if is_wide:
                    full_copy(s, k, side, is_wide).start()
                else:
                    n_full_copy(s, k, side, 1).start()
                    n_full_copy(s, k, side, 0).start()

    def three(s, k, col):
        return (
            partial[s, k - 1, :, col].astype(jnp.float32)
            + full_hi[s, :, col].astype(jnp.float32)
            + full_lo[s, :, col].astype(jnp.float32)
        )

    def deliver(s, final):
        for h in range(2):
            sib_send[s, h] = final[:, :, 256 + 128 * h:256 + 128 * (h + 1)]
        co_copy(s, core).start()
        for h in range(2):
            result[2 * s + h, :, core] = final[:, :, 128 * h:128 * (h + 1)]

    def stage3(s, k, is_wide):
        @pl.when(y == owner(k))
        def _():
            if is_wide:
                full_copy(s, k, 0, is_wide).wait_recv()
                full_copy(s, k, 1, is_wide).wait_recv()
                xsend[s] = three(s, k, 1 - xh).astype(jnp.bfloat16)
                xh_copy(s).start()
            else:
                i, part, hi, lo, _, _ = buffers(False, s)
                n_sib_copy(s, k).wait_recv()
                for other in range(2):
                    n_full_copy(s, k, 0, other).wait_recv()
                    n_full_copy(s, k, 1, other).wait_recv()
                    mine = n_sib[i] if other else part[i, k - 1, :, :, 0:256]
                    final = (
                        mine.astype(jnp.float32)
                        + hi[i, other].astype(jnp.float32)
                        + lo[i, other].astype(jnp.float32)
                    ).astype(jnp.bfloat16)
                    for h in range(2):
                        result[2 * s + h, :, 1 - core if other else core] = (
                            final[:, :, 128 * h:128 * (h + 1)]
                        )

    def stage4(s, k, is_wide):
        if is_wide:
            @pl.when(y == owner(k))
            def _():
                xh_copy(s).wait_recv()
                final = three(s, k, xh) + xrecv[s].astype(jnp.float32)
                deliver(s, final.astype(jnp.bfloat16))

    def first(s, k, is_wide):
        if is_wide:
            for direction in range(2):
                z_one(s, direction, True, True).start()

    def begin(s, k, is_wide):
        if is_wide:
            x0_copy(s, 1 - xl).wait_recv()
            for direction in range(2):
                z_one(s, direction, True, False).start()
        else:
            @pl.when(inner)
            def _():
                x0_copy(s, xh).wait_recv()

            pb_copy(s, 0, 1 - xh).wait_recv()
            z_send(s, 1, is_wide)

    def arrive(s, k, is_wide):
        z_recv(s, k, is_wide)
        if k < 4:
            z_send(s, k + 1, is_wide)
        if is_wide and k == 3:
            xf_copy(s, 0, True).start()
            xf_copy(s, 1, True).start()
        if is_wide and k == 4:
            xf_copy(s, 2, True).start()

    def multiply(s, k, is_wide):
        if k == 1:
            w_copy(s).wait_recv()
            if not is_wide:
                wf_copy(s).wait_recv()
        if is_wide and k == 3:
            xf_copy(s, 0, False).wait_recv()
            xf_copy(s, 1, False).wait_recv()
        if is_wide and k == 4:
            xf_copy(s, 2, False).wait_recv()
        stage1(s, k, is_wide)

    def send_own(s, carry):
        x0_copy(s, xl).start()
        w_copy(s).start()
        return carry

    def send_w(s, carry):
        w_copy(s).start()
        return carry

    lax.fori_loop(0, WIDE, send_own, 0)
    lax.fori_loop(WIDE, NSYM, send_w, 0)
    t2_copy.wait()

    for s in range(EARLY):
        first(s, 1, True)

    @pl.when(outer)
    def _():
        t2_narrow.wait()

    ints_copy.wait()

    actions = {
        "first": first, "begin": begin, "arrive": arrive, "multiply": multiply,
        "add": stage2, "own": stage3, "finish": stage4,
    }
    narrow_actions = {
        "rows": send_rows, "weights": send_weights, "forward": forward_weights,
    }

    def within(s, low, high, act):
        @pl.when(jnp.logical_and(s >= low, s < high))
        def _():
            act()

    def tick_body(tick, carry):
        for name, k, back in SCHEDULE:
            s = tick - back
            if name in narrow_actions:
                within(s, WIDE, NSYM, lambda: narrow_actions[name](s, k))
            else:
                within(s, 0, WIDE, lambda: actions[name](s, k, True))
                within(s, WIDE, NSYM, lambda: actions[name](s, k, False))
        return carry

    lax.fori_loop(0, NSYM + max(entry[2] for entry in SCHEDULE), tick_body, 0)

    def drain_common(s, is_wide):
        w_copy(s).wait_send()
        for direction in range(2):
            if is_wide:
                z_one(s, direction, True, True).wait_send()
                z_one(s, direction, True, False).wait_send()
            else:
                z_copy(s, 1, direction, True, is_wide).wait_send()
            for k in range(2, 5):
                z_copy(s, k, direction, True, is_wide).wait_send()
        for side in range(2):
            half_copy(s, 1, side, is_wide).wait_send()
            if is_wide:
                full_copy(s, 1, side, is_wide).wait_send()
            else:
                n_full_copy(s, 1, side, 0).wait_send()
                n_full_copy(s, 1, side, 1).wait_send()
        if is_wide:
            co_copy(s, core).wait_send()
            co_copy(s, 1 - core).wait_recv()
        else:
            n_sib_copy(s, 1).wait_send()

    def drain_wide(s, carry):
        x0_copy(s, xl).wait_send()
        for f in range(3):
            xf_copy(s, f, True).wait_send()
        xh_copy(s).wait_send()
        drain_common(s, True)
        return carry

    def drain_narrow(s, carry):
        @pl.when(outer)
        def _():
            x0_copy(s, xh).wait_send()

        @pl.when(inner)
        def _():
            pb_copy(s, 0, xh).wait_send()
            pb_copy(s, 1, xh).wait_send()

        wx_copy(s, xh).wait_send()
        wf_copy(s).wait_send()
        drain_common(s, False)
        return carry

    lax.fori_loop(0, WIDE, drain_wide, 0)
    lax.fori_loop(WIDE, NSYM, drain_narrow, 0)

    out_copy = pltpu.make_async_copy(result, out_ref, local_sem.at[0])
    out_copy.start()
    out_copy.wait()


def merge_tiles(load, first, second):
    pieces = []
    for want, tile in ((0, first), (1, second)):
        a = load(tile // 2)
        pieces.append(jnp.where(lax.rem(tile, 2) == want, a, pltpu.roll(a, 64, 1)))
    lane = lax.broadcasted_iota(jnp.int32, pieces[0].shape, 1)
    return jnp.where(lane < 64, pieces[0], pieces[1])


def sort_kernel(ab_ref, cd_ref, t2_ref, ints_ref, t2_out, ints_out, inverse_ref, order, count, sem):
    def clear(s, carry):
        count[s] = 0
        count[NSYM + s] = 0
        return carry

    lax.fori_loop(0, NSYM, clear, 0)

    def place_ab(i, carry):
        s = ab_ref[i]
        c = count[NSYM + s]
        inverse_ref[i] = s * 4 + c
        pltpu.make_async_copy(ints_ref.at[i], ints_out.at[s, c], sem).start()
        count[NSYM + s] = c + 1
        return carry

    lax.fori_loop(0, 32, place_ab, 0, unroll=4)
    def place_cd(i, carry):
        s = cd_ref[i]
        c = count[s]
        order[s * 8 + c] = i
        count[s] = c + 1
        return carry

    lax.fori_loop(0, 64, place_cd, 0, unroll=4)

    whole = pltpu.make_async_copy(ints_out, ints_out, sem)

    def load(chunk):
        return t2_ref[:, pl.ds(pl.multiple_of(chunk * 128, 128), 128)]

    def sort_t2(s, carry):
        for j in range(K // 128):
            t2_out[s, :, 128 * j:128 * (j + 1)] = merge_tiles(
                load, order[s * 8 + 2 * j], order[s * 8 + 2 * j + 1]
            )
        return carry

    lax.fori_loop(0, NSYM, sort_t2, 0)
    whole.wait()


def unsort_kernel(inverse_ref, sorted_ref, out_ref):
    for p in range(16):
        out_ref[:, 128 * p:128 * (p + 1)] = merge_tiles(
            lambda chunk: sorted_ref[chunk], inverse_ref[2 * p], inverse_ref[2 * p + 1]
        )


def per_device(t2_amps, integrals, ab_sym, cd_sym):
    bf16 = jnp.bfloat16
    dma = pltpu.SemaphoreType.DMA
    smem = pl.BlockSpec(memory_space=pltpu.SMEM)
    vmem = pl.BlockSpec(memory_space=pltpu.VMEM)
    hbm = pl.BlockSpec(memory_space=pltpu.HBM)
    t2_sorted, ints_sorted, inverse = pl.pallas_call(
        sort_kernel,
        out_shape=(
            jax.ShapeDtypeStruct((NSYM, ROWS, K), bf16),
            jax.ShapeDtypeStruct((NSYM, 4, 64, K), bf16),
            jax.ShapeDtypeStruct((32,), jnp.int32),
        ),
        in_specs=[smem, smem, vmem, hbm],
        out_specs=(vmem, vmem, smem),
        scratch_shapes=[pltpu.SMEM((64,), jnp.int32), pltpu.SMEM((16,), jnp.int32), dma(())],
    )(ab_sym, cd_sym, t2_amps, integrals)
    result = pl.pallas_call(
        kernel,
        out_shape=jax.ShapeDtypeStruct((2 * NSYM, 2, 2, ROWS, 128), bf16),
        in_specs=[hbm, hbm],
        out_specs=hbm,
        scratch_shapes=[
            pltpu.VMEM((NSYM, NZ, 2, ROWS, K), bf16),
            pltpu.VMEM((NSYM, 2, 512, K), bf16),
            pltpu.VMEM((WIDE, 4, 2, 2, ROWS, 512), bf16),
            pltpu.VMEM((WIDE, 2, 2, ROWS, 512), bf16),
            pltpu.VMEM((WIDE, 2, 2, ROWS, 512), bf16),
            pltpu.VMEM((WIDE, 2, ROWS, 512), bf16),
            pltpu.VMEM((WIDE, 2, ROWS, 512), bf16),
            pltpu.VMEM((WIDE, 2, ROWS, 512), bf16),
            pltpu.VMEM((WIDE, 2, ROWS, 512), bf16),
            pltpu.VMEM((NARROW, 4, 2, ROWS, 512), bf16),
            pltpu.VMEM((NARROW, 2, 2, ROWS, 256), bf16),
            pltpu.VMEM((NARROW, 2, 2, ROWS, 256), bf16),
            pltpu.VMEM((NARROW, ROWS, 512), bf16),
            pltpu.VMEM((NARROW, ROWS, 512), bf16),
            pltpu.VMEM((NARROW, 2, ROWS, 256), bf16),
            pltpu.VMEM((NSYM, 2, 2, ROWS, 128), bf16),
            pltpu.VMEM((2 * NSYM, 2, 2, ROWS, 128), bf16),
            dma((3,)),
            dma((NSYM,)), dma((NSYM,)),
            dma((NSYM,)), dma((NSYM,)),
            dma((5, 2, NSYM)), dma((5, 2, NSYM)),
            dma((3, NSYM)), dma((3, NSYM)),
            dma((2, NSYM)), dma((2, NSYM)),
            dma((4, NSYM)), dma((4, NSYM)),
            dma((NSYM,)), dma((NSYM,)),
            dma((NSYM,)), dma((NSYM,)),
            dma((NSYM,)), dma((NSYM,)),
            dma((NSYM,)), dma((NSYM,)),
            dma((2, NSYM)), dma((NSYM,)),
        ],
        compiler_params=pltpu.CompilerParams(
            collective_id=0, has_side_effects=True, vmem_limit_bytes=62 << 20
        ),
    )(t2_sorted, ints_sorted.reshape(NSYM, 256, K))
    return pl.pallas_call(
        unsort_kernel,
        out_shape=jax.ShapeDtypeStruct((256, 2048), bf16),
        in_specs=[smem, vmem],
        out_specs=vmem,
    )(inverse, result.reshape(2 * NSYM, 256, 128))


def solution(mesh):
    in_specs = (P("blk", "cd"), P("blk", None, "cd"), P("blk"), P("cd"))
    out_specs = P("cd", "blk")
    return jax.shard_map(
        per_device, mesh=mesh, in_specs=in_specs, out_specs=out_specs, check_vma=False
    )
```

time: 128 us -> 113 us (0.88)
  Pallas kernels: 127 us -> 112 us
    pallas_call x1, Pallas kernels: 118 us -> 105 us  [per_device(): pl.pallas_call(kernel, out_shape=jax.ShapeDtypeStruct((2 * NSYM, 2, 2, RO...]
where the time goes in v3:
time: 113 us; the launch traced here: 112 us
  Pallas kernels  112 us (99%)
    pallas_call x1, Pallas kernels, per_device(): pl.pallas_call(kernel, out_shape=jax.ShapeDtypeStruct((2 * NSYM, 2, 2, RO...  105 us
    pallas_call x1, Pallas kernels, per_device(): pl.pallas_call(sort_kernel, out_shape=(jax.ShapeDtypeStruct((NSYM, ROWS,...  4.24 us
    pallas_call x1, Pallas kernels, per_device(): pl.pallas_call(unsort_kernel, out_shape=jax.ShapeDtypeStruct((256, 2048),...  2.9 us

profile of v3, /device:TPU:17, one launch (start us, length us, event | category | flops | bytes accessed | tf_op | source)
XLA Modules:
  0.0 112.2 jit_solution(10147365024886925539)
XLA Ops:
  0.0 4.2 %shard_map.46 = (bf16[8,64,512]{2,1,0:T(8,128)(2,1)}, bf16[8,4,64,512]{3,2,1,0:T(8,128)(2,1)}, s32[32]{0:T(128)}) custom-call(s32[32]{0:T(128)} %ab_ref.1, s32[64]{0:T(128)} %cd_ref.1, bf16[64,4096]{1,0:T(8,128)(2,1)} %t2_ref.1, bf16[32,64,512]{2,1,0:T(8,128)(2,1)} %ints_ref.1), custom_call_target="tpu_custom_call" | custom-call | tf_op jit(solution)/shard_map/pallas_call | solution.py:524
  4.2 105.1 %shard_map.47 = bf16[16,2,2,64,128]{4,3,2,1,0:T(8,128)(2,1)} custom-call(bf16[8,64,512]{2,1,0:T(8,128)(2,1)} %get-tuple-element.9.t2_ref, bf16[8,256,512]{2,1,0:T(8,128)(2,1)} %bitcast.3), custom_call_target="tpu_custom_call" | custom-call | tf_op jit(solution)/shard_map/pallas_call | solution.py:535
  109.3 2.9 %shard_map.48 = bf16[256,2048]{1,0:T(8,128)(2,1)} custom-call(s32[32]{0:T(128)} %get-tuple-element.8.inverse_ref, bf16[16,256,128]{2,1,0:T(8,128)(2,1)} %bitcast.2), custom_call_target="tpu_custom_call" | custom-call | tf_op jit(solution)/shard_map/pallas_call | solution.py:575

commit v4 on v3

--- a/solution.py
+++ b/solution.py
@@ -16,30 +16,30 @@
 EARLY = 2
 SCHEDULE = (
     ("begin", 0, 0),
+    ("finish", 4, 6),
+    ("own", 4, 5),
+    ("arrive", 2, 1),
+    ("add", 2, 2),
+    ("multiply", 2, 1),
     ("add", 3, 3),
-    ("arrive", 2, 1),
     ("arrive", 4, 2),
     ("multiply", 3, 2),
-    ("add", 2, 2),
-    ("multiply", 2, 1),
-    ("finish", 3, 5),
-    ("own", 3, 4),
     ("finish", 2, 4),
     ("own", 2, 3),
     ("forward", 0, -2),
     ("arrive", 1, 0),
     ("rows", 0, -6),
+    ("finish", 3, 5),
+    ("own", 3, 4),
     ("add", 1, 1),
-    ("add", 4, 3),
+    ("multiply", 1, 0),
     ("arrive", 3, 1),
-    ("multiply", 1, 0),
-    ("multiply", 4, 2),
     ("weights", 0, -6),
     ("finish", 1, 3),
-    ("finish", 4, 5),
     ("own", 1, 2),
-    ("own", 4, 4),
     ("first", 1, -2),
+    ("add", 4, 3),
+    ("multiply", 4, 2),
 )
 
 
@@ -391,18 +391,6 @@
         def _():
             act()
 
-    def tick_body(tick, carry):
-        for name, k, back in SCHEDULE:
-            s = tick - back
-            if name in narrow_actions:
-                within(s, WIDE, NSYM, lambda: narrow_actions[name](s, k))
-            else:
-                within(s, 0, WIDE, lambda: actions[name](s, k, True))
-                within(s, WIDE, NSYM, lambda: actions[name](s, k, False))
-        return carry
-
-    lax.fori_loop(0, NSYM + max(entry[2] for entry in SCHEDULE), tick_body, 0)
-
     def drain_common(s, is_wide):
         w_copy(s).wait_send()
         for direction in range(2):
@@ -422,19 +410,17 @@
                 n_full_copy(s, 1, side, 1).wait_send()
         if is_wide:
             co_copy(s, core).wait_send()
-            co_copy(s, 1 - core).wait_recv()
         else:
             n_sib_copy(s, 1).wait_send()
 
-    def drain_wide(s, carry):
+    def drain_wide(s):
         x0_copy(s, xl).wait_send()
         for f in range(3):
             xf_copy(s, f, True).wait_send()
         xh_copy(s).wait_send()
         drain_common(s, True)
-        return carry
-
-    def drain_narrow(s, carry):
+
+    def drain_narrow(s):
         @pl.when(outer)
         def _():
             x0_copy(s, xh).wait_send()
@@ -447,14 +433,36 @@
         wx_copy(s, xh).wait_send()
         wf_copy(s).wait_send()
         drain_common(s, False)
-        return carry
-
-    lax.fori_loop(0, WIDE, drain_wide, 0)
-    lax.fori_loop(WIDE, NSYM, drain_narrow, 0)
-
-    out_copy = pltpu.make_async_copy(result, out_ref, local_sem.at[0])
-    out_copy.start()
-    out_copy.wait()
+
+    def out_copy(s):
+        part = pl.ds(2 * s, 2)
+        return pltpu.make_async_copy(result.at[part], out_ref.at[part], local_sem.at[3 + s])
+
+    def write_out(s):
+        co_copy(s, 1 - core).wait_recv()
+        out_copy(s).start()
+
+    def tick_body(tick, carry):
+        for name, k, back in SCHEDULE:
+            s = tick - back
+            if name in narrow_actions:
+                within(s, WIDE, NSYM, lambda: narrow_actions[name](s, k))
+            else:
+                within(s, 0, WIDE, lambda: actions[name](s, k, True))
+                within(s, WIDE, NSYM, lambda: actions[name](s, k, False))
+        within(tick - last, 0, WIDE, lambda: drain_wide(tick - last))
+        within(tick - last, WIDE, NSYM, lambda: drain_narrow(tick - last))
+        within(tick - last - 1, 0, WIDE, lambda: write_out(tick - last - 1))
+        return carry
+
+    last = max(entry[2] for entry in SCHEDULE)
+
+    lax.fori_loop(0, NSYM + last, tick_body, 0)
+
+    for s in range(WIDE, NSYM):
+        out_copy(s).start()
+    for s in range(NSYM):
+        out_copy(s).wait()
 
 
 def merge_tiles(load, first, second):
@@ -555,7 +563,7 @@
             pltpu.VMEM((NARROW, 2, ROWS, 256), bf16),
             pltpu.VMEM((NSYM, 2, 2, ROWS, 128), bf16),
             pltpu.VMEM((2 * NSYM, 2, 2, ROWS, 128), bf16),
-            dma((3,)),
+            dma((3 + NSYM,)),
             dma((NSYM,)), dma((NSYM,)),
             dma((NSYM,)), dma((NSYM,)),
             dma((5, 2, NSYM)), dma((5, 2, NSYM)),

time: 113 us -> 113 us (level)
  no operation moved by 1% of the time
where the time goes in v4:
time: 113 us; the launch traced here: 112 us
  Pallas kernels  112 us (99%)
    pallas_call x1, Pallas kernels, per_device(): pl.pallas_call(kernel, out_shape=jax.ShapeDtypeStruct((2 * NSYM, 2, 2, RO...  105 us
    pallas_call x1, Pallas kernels, per_device(): pl.pallas_call(sort_kernel, out_shape=(jax.ShapeDtypeStruct((NSYM, ROWS,...  4.24 us
    pallas_call x1, Pallas kernels, per_device(): pl.pallas_call(unsort_kernel, out_shape=jax.ShapeDtypeStruct((256, 2048),...  2.9 us

profile of v4, /device:TPU:17, one launch (start us, length us, event | category | flops | bytes accessed | tf_op | source)
XLA Modules:
  0.0 111.9 jit_solution(10044924430797630473)
XLA Ops:
  0.0 4.2 %shard_map.46 = (bf16[8,64,512]{2,1,0:T(8,128)(2,1)}, bf16[8,4,64,512]{3,2,1,0:T(8,128)(2,1)}, s32[32]{0:T(128)}) custom-call(s32[32]{0:T(128)} %ab_ref.1, s32[64]{0:T(128)} %cd_ref.1, bf16[64,4096]{1,0:T(8,128)(2,1)} %t2_ref.1, bf16[32,64,512]{2,1,0:T(8,128)(2,1)} %ints_ref.1), custom_call_target="tpu_custom_call" | custom-call | tf_op jit(solution)/shard_map/pallas_call | solution.py:532
  4.2 104.8 %shard_map.47 = bf16[16,2,2,64,128]{4,3,2,1,0:T(8,128)(2,1)} custom-call(bf16[8,64,512]{2,1,0:T(8,128)(2,1)} %get-tuple-element.9.t2_ref, bf16[8,256,512]{2,1,0:T(8,128)(2,1)} %bitcast.3), custom_call_target="tpu_custom_call" | custom-call | tf_op jit(solution)/shard_map/pallas_call | solution.py:543
  109.0 2.9 %shard_map.48 = bf16[256,2048]{1,0:T(8,128)(2,1)} custom-call(s32[32]{0:T(128)} %get-tuple-element.8.inverse_ref, bf16[16,256,128]{2,1,0:T(8,128)(2,1)} %bitcast.2), custom_call_target="tpu_custom_call" | custom-call | tf_op jit(solution)/shard_map/pallas_call | solution.py:583
